TPU v7x, 32 devices: a whole 2x2x4 slice. The times are simulated.
32 devices in a mesh: req: 4 (over z), tok: 8 (over y, x, core).
Axes of the slice: x: 2, y: 2, z: 4, core: 2. Of those that a mesh axis runs over, the one named last changes fastest.
Arguments:
- hidden_in: bfloat16 [4096, 2048], P(('req', 'tok')), may hold values from -1.5 to 1.5
- suffix_len: int32 [4, 4], P('req'), may hold values from 1 to 512, 1024 in all within a row
- prefix_of: int32 [4, 4], P('req'), may hold values from 0 to 3
- prefix_slot: int32 [4], replicated, may hold values from 0 to 3, each once
- prefix_cache: bfloat16 [4, 4, 2048, 128], P('req', None, 'tok'), may hold values from -160 to 160
- attn_gain: bfloat16 [2048], replicated, may hold values from 0.099609375 to 1.8984375
- query_weight: bfloat16 [2048, 2048], P(None, 'tok'), may hold values from -0.125 to 0.125
- keyval_weight: bfloat16 [4, 2048, 128], replicated, may hold values from -0.125 to 0.125
- out_weight: bfloat16 [2048, 2048], P('tok'), may hold values from -0.125 to 0.125
- mlp_gain: bfloat16 [2048], replicated, may hold values from 0.099609375 to 1.8984375
- gate_weight: bfloat16 [2048, 4096], P(None, 'req'), may hold values from -0.125 to 0.125
- up_weight: bfloat16 [2048, 4096], P(None, 'req'), may hold values from -0.125 to 0.125
- down_weight: bfloat16 [4096, 2048], P('req'), may hold values from -0.09375 to 0.09375
- final_gain: bfloat16 [2048], replicated, may hold values from 0.099609375 to 1.8984375
- head_weight: bfloat16 [32000, 2048], P('tok'), may hold values from -7 to 7
Outputs:
- hidden_out: bfloat16 [4096, 2048], P(('req', 'tok'))
- suffix_cache: bfloat16 [4096, 512], P('req', 'tok')
- last_rms: float32 [4, 4], P('req')
- top_logit: float32 [4, 4], P('req')
- log_total: float32 [4, 4], P('req')
Inputs may be any that keep to these rules, and one draw needn't show every extreme that they name: `suffix_len`: each owner's 4 lengths sum to 1024, and the largest of each owner is 512.
All inputs are finite; a program needn't handle non-finite values.
Results may differ from a plain program's by a relative error of at most 0.02.
Values may be sent and summed in bfloat16 or wider, within the bound.
A program may use at most 128 MiB of HBM per device.

v0:
```python
import math

import jax
import jax.numpy as jnp
from jax import lax
from jax.sharding import PartitionSpec as P

HD = 64
PRE_LEN = 16384


epsilon = 1e-05
neg_large = -1e30


def rms_scale(values, gain_vec):
    widened = values.astype(jnp.float32)
    mean_square = jnp.mean(widened * widened, axis=-1, keepdims=True)
    return widened * lax.rsqrt(mean_square + epsilon) * gain_vec.astype(jnp.float32)


def rotate(vectors, positions):
    half_width = vectors.shape[-1] // 2
    levels = jnp.arange(half_width).astype(jnp.float32)
    inverse = jnp.exp(levels * (-2.0 * math.log(10000.0) / vectors.shape[-1]))
    angles = positions.astype(jnp.float32)[:, None] * inverse[None, :]
    cosine = jnp.cos(angles)[:, None, :]
    sine_part = jnp.sin(angles)[:, None, :]
    first_half = vectors[..., :half_width]
    second_half = vectors[..., half_width:]
    return jnp.concatenate(
        [
            first_half * cosine - second_half * sine_part,
            second_half * cosine + first_half * sine_part,
        ],
        axis=-1,
    )


def owner_layout(lengths, row_count):
    end_rows = jnp.cumsum(lengths)
    starts = end_rows - lengths
    row_index = jnp.arange(row_count)
    member = (row_index[:, None] >= starts[None, :]) & (row_index[:, None] < end_rows[None, :])
    offsets = row_index - jnp.sum(jnp.where(member, starts[None, :], 0), axis=1)
    return (starts, end_rows, offsets)


def slot_lookup(chosen, prefix_slot):
    table_index = jnp.arange(prefix_slot.shape[0])
    hits = chosen[:, None] == table_index[None, :]
    return jnp.sum(jnp.where(hits, prefix_slot[None, :], 0), axis=1)


def request_attention(query_block, suffix_block, window, live_len):
    row_count = query_block.shape[0]
    head_width = query_block.shape[-1]
    window_len = window.shape[1]
    suffix_major = jnp.transpose(suffix_block, (1, 0, 2))
    key_rows = jnp.concatenate([window[:, :, :head_width], suffix_major[:, :, :head_width]], axis=1)
    value_rows = jnp.concatenate(
        [window[:, :, head_width:], suffix_major[:, :, head_width:]], axis=1
    )
    scores = jnp.einsum(
        "rgke,gse->gkrs", query_block, key_rows, preferred_element_type=jnp.float32
    ) * head_width ** (-0.5)
    row_index = jnp.arange(row_count)
    prefix_seen = jnp.arange(window_len)[None, :] > row_index[:, None]
    suffix_seen = (
        (row_index[None, :] <= row_index[:, None])
        & (row_index[:, None] - row_index[None, :] < window_len)
        & (row_index[None, :] < live_len)
    )
    visible = jnp.concatenate([prefix_seen, suffix_seen], axis=1)
    masked = jnp.where(visible, scores, neg_large)
    highest = jnp.max(masked, axis=-1, keepdims=True)
    weights = jnp.where(visible, jnp.exp(masked - highest), 0.0)
    totals = jnp.sum(weights, axis=-1, keepdims=True)
    totals = jnp.where(row_index[:, None] < live_len, totals, 1.0)
    rounded = weights.astype(jnp.bfloat16)
    mixed_rows = jnp.einsum(
        "gkrs,gse->rgke", rounded, value_rows, preferred_element_type=jnp.float32
    )
    mixed_rows = mixed_rows / jnp.transpose(totals, (2, 0, 1, 3))
    return mixed_rows.reshape(row_count, -1).astype(jnp.bfloat16)


def shards(
    hidden_in,
    suffix_len,
    prefix_of,
    prefix_slot,
    prefix_cache,
    attn_gain,
    query_weight,
    keyval_weight,
    out_weight,
    mlp_gain,
    gate_weight,
    up_weight,
    down_weight,
    final_gain,
    head_weight,
):
    tok_count = lax.axis_size("tok")
    tok_place = lax.axis_index("tok")
    tok_rows = hidden_in.shape[0]
    own_rows = tok_rows * tok_count
    most_rows = own_rows // 2
    heads_here = query_weight.shape[1] // HD
    kv_count = keyval_weight.shape[0]
    kv_head = tok_place * kv_count // tok_count
    repeat_count = tok_count // kv_count
    lengths = suffix_len[0]
    starts, end_rows, offsets = owner_layout(lengths, own_rows)
    positions = offsets + PRE_LEN
    normed = rms_scale(hidden_in, attn_gain).astype(jnp.bfloat16)
    kv_weight = lax.dynamic_index_in_dim(keyval_weight, kv_head, 0, keepdims=False)
    united_weight = jnp.concatenate([query_weight, kv_weight], axis=1)
    projected = jnp.dot(
        lax.all_gather(normed, "tok", axis=0, tiled=True),
        united_weight,
        preferred_element_type=jnp.float32,
    )
    queries = rotate(
        projected[:, : heads_here * HD].reshape(own_rows, heads_here, HD), positions
    ).astype(jnp.bfloat16)
    keyvals = projected[:, heads_here * HD :].reshape(own_rows, 1, 2 * HD)
    rotated = rotate(keyvals[:, :, :HD], positions)
    keyvals = jnp.concatenate([rotated, keyvals[:, :, HD:]], axis=-1).astype(jnp.bfloat16)
    cache_width = kv_count * 2 * HD // tok_count
    cache_offset = tok_place * cache_width % (2 * HD)
    suffix_cache = lax.dynamic_slice_in_dim(keyvals[:, 0, :], cache_offset, cache_width, 1)
    every_owner = lax.all_gather(prefix_cache, "req", axis=0, tiled=True)
    routed = jnp.repeat(every_owner, repeat_count, axis=1)
    windows = lax.all_to_all(routed, "tok", split_axis=1, concat_axis=2, tiled=True)
    windows = windows[:, 0]
    padded_queries = jnp.concatenate(
        [queries, jnp.zeros((most_rows, heads_here, HD), jnp.bfloat16)], axis=0
    )
    padded_keyvals = jnp.concatenate(
        [keyvals, jnp.zeros((most_rows, 1, 2 * HD), jnp.bfloat16)], axis=0
    )
    cache_rows = slot_lookup(prefix_of[0], prefix_slot)

    def one_request(buffer, request):
        first_row, live_len, cache_row = request
        query_block = lax.dynamic_slice_in_dim(padded_queries, first_row, most_rows, 0).reshape(
            most_rows, 1, heads_here, HD
        )
        suffix_block = lax.dynamic_slice_in_dim(padded_keyvals, first_row, most_rows, 0)
        window = lax.dynamic_index_in_dim(windows, cache_row, 0, keepdims=True)
        mixed_rows = request_attention(query_block, suffix_block, window, live_len)
        current = lax.dynamic_slice_in_dim(buffer, first_row, most_rows, 0)
        keep_rows = jnp.arange(most_rows)[:, None] < live_len
        return (
            lax.dynamic_update_slice_in_dim(
                buffer, jnp.where(keep_rows, mixed_rows, current), first_row, 0
            ),
            None,
        )

    buffer = jnp.zeros((own_rows + most_rows, heads_here * HD), jnp.bfloat16)
    buffer, unused = lax.scan(one_request, buffer, (starts, lengths, cache_rows))
    attended = buffer[:own_rows]
    projected_back = lax.psum_scatter(
        jnp.dot(attended, out_weight, preferred_element_type=jnp.float32).astype(jnp.bfloat16),
        "tok",
        scatter_dimension=0,
        tiled=True,
    ).astype(jnp.float32)
    middle = (hidden_in.astype(jnp.float32) + projected_back).astype(jnp.bfloat16)
    mlp_in = rms_scale(middle, mlp_gain).astype(jnp.bfloat16)
    shard_part = lax.all_gather(mlp_in, "req", axis=0, tiled=True)
    gate_proj = jnp.dot(shard_part, gate_weight, preferred_element_type=jnp.float32)
    lifted = jnp.dot(shard_part, up_weight, preferred_element_type=jnp.float32)
    hidden_act = (jax.nn.silu(gate_proj) * lifted).astype(jnp.bfloat16)
    summed = lax.psum_scatter(
        jnp.dot(hidden_act, down_weight, preferred_element_type=jnp.float32).astype(jnp.bfloat16),
        "req",
        scatter_dimension=0,
        tiled=True,
    ).astype(jnp.float32)
    final_state = (middle.astype(jnp.float32) + summed).astype(jnp.bfloat16)
    local_index = jnp.arange(tok_rows) + tok_place * tok_rows
    picker = (local_index[None, :] == (end_rows - 1)[:, None]).astype(jnp.bfloat16)
    picked = jnp.dot(picker, final_state, preferred_element_type=jnp.float32)
    last_rows = lax.psum(picked.astype(jnp.bfloat16), "tok").astype(jnp.float32)
    mean_square = jnp.mean(last_rows * last_rows, axis=-1, keepdims=True)
    spread = jnp.sqrt(mean_square + epsilon)
    final_normed = (
        last_rows * lax.rsqrt(mean_square + epsilon) * final_gain.astype(jnp.float32)
    ).astype(jnp.bfloat16)
    logits = lax.dot_general(
        final_normed, head_weight, (((1,), (1,)), ((), ())), preferred_element_type=jnp.float32
    )
    highest = lax.pmax(jnp.max(logits, axis=-1), "tok")
    summed_exp = lax.psum(jnp.sum(jnp.exp(logits - highest[:, None]), axis=-1), "tok")
    log_total = highest + jnp.log(summed_exp)
    return (final_state, suffix_cache, spread[:, 0][None, :], highest[None, :], log_total[None, :])


def solution(mesh):
    placed = (
        P(("req", "tok"), None),
        P("req", None),
        P("req", None),
        P(),
        P("req", None, "tok", None),
        P(),
        P(None, "tok"),
        P(),
        P("tok", None),
        P(),
        P(None, "req"),
        P(None, "req"),
        P("req", None),
        P(),
        P("tok", None),
    )
    return jax.shard_map(
        shards,
        mesh=mesh,
        in_specs=placed,
        out_specs=(
            P(("req", "tok"), None),
            P("req", "tok"),
            P("req", None),
            P("req", None),
            P("req", None),
        ),
        check_vma=False,
    )
```

profile of v0, /device:TPU:9, one launch (start us, length us, event | category | flops | bytes accessed | tf_op | source)
XLA Modules:
  0.0 458.5 jit_solution(11795564161702369459)
XLA Ops:
  11.9 26.5 %all-gather.4.cloned.1.call-done = bf16[4,4,256,128]{3,2,1,0:T(8,128)(2,1)} async-done(((bf16[1,4,256,128]{3,2,1,0:T(8,128)(2,1)}), bf16[4,4,256,128]{3,2,1,0:T(8,128)(2,1)}) %all-gather.4.cloned.1.call-update) | async-done | bytes 1048592 | tf_op jit(solution)/shard_map/all_gather | solution.py:134
  41.6 5.1 %all-to-all-start = ((bf16[4,8,256,128]{2,3,0,1:T(8,128)(2,1)}), bf16[4,8,256,128]{2,3,0,1:T(8,128)(2,1)}, u32[]{:S(2)}, u32[]{:S(2)}) async-start(bf16[4,8,256,128]{2,3,0,1:T(8,128)(2,1)} %bitcast.128), calls=%async_computation | async-start | bytes 4194304 | tf_op jit(solution)/shard_map/all_to_all | solution.py:136
  50.8 24.8 %all-to-all-done = bf16[4,8,256,128]{2,3,0,1:T(8,128)(2,1)} async-done(((bf16[4,8,256,128]{2,3,0,1:T(8,128)(2,1)}), bf16[4,8,256,128]{2,3,0,1:T(8,128)(2,1)}, u32[]{:S(2)}, u32[]{:S(2)}) %all-to-all-start) | async-done | bytes 2097184 | tf_op jit(solution)/shard_map/all_to_all | solution.py:136
  75.6 3.0 copy.30
  78.6 13.1 %all-gather.6.cloned.1.call-done = bf16[1024,2048]{1,0:T(8,128)(2,1)} async-done(((bf16[128,2048]{1,0:T(8,128)(2,1)}), bf16[1024,2048]{1,0:T(8,128)(2,1)}) %all-gather.6.cloned.1.call-update) | async-done | bytes 4194320 | tf_op jit(solution)/shard_map/all_gather | solution.py:121
  91.7 4.3 fusion.34
  100.3 129.7 %while.10 = (s32[]{:T(128)}, bf16[1536,256]{0,1:T(8,128)(2,1)}, s32[4]{0:T(128)}, s32[4]{0:T(128)}, bf16[4,2048,128]{2,1,0:T(8,128)(2,1)S(1)}, /*index=5*/s32[4]...) while((s32[]{:T(128)}, bf16[1536,256]{0,1:T(8,128)(2,1)}, ...), condition=%wide.region_7.8_spmd, body=%wide.region_4.7_spmd.sunk | while | flops 1415707136 | bytes 83556792 | solution.py:164
  112.5 4.7 %fusion.93 = (f32[4,512]{1,0:T(4,128)S(1)}, f32[2560,512,4]{1,0,2:T(8,128)S(1)}) fusion(pred[512,2560]{0,1:T(8,128)(4,1)S(1)} %pad_add_fusion.2, bf16[1536,4,64]{0,2,1:T(8,128)(2,1)} %get-tuple-element.192, s32[]{:T(128)S(6)} %select_n.119, bf16[1,512,64]{1,2,0:T(8,128)(2,1)S(1)} %copy-done.10, bf16[1,2048,64]{1,2,0:T(8,128)(2,1)S(1)} %copy-done.5), kind=kOutput, calls=%fused_computation.2.clone.1 | convolution fusion | flops 687470592 | bytes 22880260 | tf_op jit(solution)/shard_map/while/body/eval_jaxpr/rgke,gse->gkrs/dot_general | solution.py:64
  117.2 5.2 %fusion.94 = f32[4,512]{1,0:T(4,128)S(1)} fusion(f32[2560,512,4]{1,0,2:T(8,128)S(1)} %get-tuple-element.155, f32[4,512]{1,0:T(4,128)S(1)} %get-tuple-element.156, pred[512,2560]{0,1:T(8,128)(4,1)S(1)} %pad_add_fusion.2), kind=kLoop, calls=%fused_computation.3.clone.1 | loop fusion | flops 26212352 | bytes 22298624 | tf_op jit(solution)/shard_map/while/body/eval_jaxpr/reduce_sum | solution.py:78
  122.4 5.9 %fusion.96 = bf16[512,1,4,64]{0,3,2,1:T(8,128)(2,1)S(1)} fusion(f32[2560,512,4]{1,0,2:T(8,128)S(1)} %get-tuple-element.155, f32[4,512]{1,0:T(4,128)S(1)} %get-tuple-element.156, pred[512,2560]{0,1:T(8,128)(4,1)S(1)} %pad_add_fusion.2, bf16[1,512,64]{1,2,0:T(8,128)(2,1)S(1)} %get-tuple-element.157, bf16[1,2048,64]{1,2,0:T(8,128)(2,1)S(1)} %copy.39, ...), kind=kOutput, calls=%fused_computation.17.clone.1 | convolution fusion | flops 698220544 | bytes 22888448 | tf_op jit(solution)/shard_map/while/body/eval_jaxpr/gkrs,gse->rgke/dot_general | solution.py:81
  129.1 2.5 dynamic_update_slice.4
  144.6 4.7 %fusion.93 = (f32[4,512]{1,0:T(4,128)S(1)}, f32[2560,512,4]{1,0,2:T(8,128)S(1)}) fusion(pred[512,2560]{0,1:T(8,128)(4,1)S(1)} %pad_add_fusion.2, bf16[1536,4,64]{0,2,1:T(8,128)(2,1)} %get-tuple-element.192, s32[]{:T(128)S(6)} %select_n.119, bf16[1,512,64]{1,2,0:T(8,128)(2,1)S(1)} %copy-done.10, bf16[1,2048,64]{1,2,0:T(8,128)(2,1)S(1)} %copy-done.5), kind=kOutput, calls=%fused_computation.2.clone.1 | convolution fusion | flops 687470592 | bytes 22880260 | tf_op jit(solution)/shard_map/while/body/eval_jaxpr/rgke,gse->gkrs/dot_general | solution.py:64
  149.3 5.2 %fusion.94 = f32[4,512]{1,0:T(4,128)S(1)} fusion(f32[2560,512,4]{1,0,2:T(8,128)S(1)} %get-tuple-element.155, f32[4,512]{1,0:T(4,128)S(1)} %get-tuple-element.156, pred[512,2560]{0,1:T(8,128)(4,1)S(1)} %pad_add_fusion.2), kind=kLoop, calls=%fused_computation.3.clone.1 | loop fusion | flops 26212352 | bytes 22298624 | tf_op jit(solution)/shard_map/while/body/eval_jaxpr/reduce_sum | solution.py:78
  154.6 5.9 %fusion.96 = bf16[512,1,4,64]{0,3,2,1:T(8,128)(2,1)S(1)} fusion(f32[2560,512,4]{1,0,2:T(8,128)S(1)} %get-tuple-element.155, f32[4,512]{1,0:T(4,128)S(1)} %get-tuple-element.156, pred[512,2560]{0,1:T(8,128)(4,1)S(1)} %pad_add_fusion.2, bf16[1,512,64]{1,2,0:T(8,128)(2,1)S(1)} %get-tuple-element.157, bf16[1,2048,64]{1,2,0:T(8,128)(2,1)S(1)} %copy.39, ...), kind=kOutput, calls=%fused_computation.17.clone.1 | convolution fusion | flops 698220544 | bytes 22888448 | tf_op jit(solution)/shard_map/while/body/eval_jaxpr/gkrs,gse->rgke/dot_general | solution.py:81
  161.3 3.1 dynamic_update_slice.4
  177.4 4.7 %fusion.93 = (f32[4,512]{1,0:T(4,128)S(1)}, f32[2560,512,4]{1,0,2:T(8,128)S(1)}) fusion(pred[512,2560]{0,1:T(8,128)(4,1)S(1)} %pad_add_fusion.2, bf16[1536,4,64]{0,2,1:T(8,128)(2,1)} %get-tuple-element.192, s32[]{:T(128)S(6)} %select_n.119, bf16[1,512,64]{1,2,0:T(8,128)(2,1)S(1)} %copy-done.10, bf16[1,2048,64]{1,2,0:T(8,128)(2,1)S(1)} %copy-done.5), kind=kOutput, calls=%fused_computation.2.clone.1 | convolution fusion | flops 687470592 | bytes 22880260 | tf_op jit(solution)/shard_map/while/body/eval_jaxpr/rgke,gse->gkrs/dot_general | solution.py:64
  182.1 5.2 %fusion.94 = f32[4,512]{1,0:T(4,128)S(1)} fusion(f32[2560,512,4]{1,0,2:T(8,128)S(1)} %get-tuple-element.155, f32[4,512]{1,0:T(4,128)S(1)} %get-tuple-element.156, pred[512,2560]{0,1:T(8,128)(4,1)S(1)} %pad_add_fusion.2), kind=kLoop, calls=%fused_computation.3.clone.1 | loop fusion | flops 26212352 | bytes 22298624 | tf_op jit(solution)/shard_map/while/body/eval_jaxpr/reduce_sum | solution.py:78
  187.4 5.9 %fusion.96 = bf16[512,1,4,64]{0,3,2,1:T(8,128)(2,1)S(1)} fusion(f32[2560,512,4]{1,0,2:T(8,128)S(1)} %get-tuple-element.155, f32[4,512]{1,0:T(4,128)S(1)} %get-tuple-element.156, pred[512,2560]{0,1:T(8,128)(4,1)S(1)} %pad_add_fusion.2, bf16[1,512,64]{1,2,0:T(8,128)(2,1)S(1)} %get-tuple-element.157, bf16[1,2048,64]{1,2,0:T(8,128)(2,1)S(1)} %copy.39, ...), kind=kOutput, calls=%fused_computation.17.clone.1 | convolution fusion | flops 698220544 | bytes 22888448 | tf_op jit(solution)/shard_map/while/body/eval_jaxpr/gkrs,gse->rgke/dot_general | solution.py:81
  194.1 3.1 dynamic_update_slice.4
  210.2 4.7 %fusion.93 = (f32[4,512]{1,0:T(4,128)S(1)}, f32[2560,512,4]{1,0,2:T(8,128)S(1)}) fusion(pred[512,2560]{0,1:T(8,128)(4,1)S(1)} %pad_add_fusion.2, bf16[1536,4,64]{0,2,1:T(8,128)(2,1)} %get-tuple-element.192, s32[]{:T(128)S(6)} %select_n.119, bf16[1,512,64]{1,2,0:T(8,128)(2,1)S(1)} %copy-done.10, bf16[1,2048,64]{1,2,0:T(8,128)(2,1)S(1)} %copy-done.5), kind=kOutput, calls=%fused_computation.2.clone.1 | convolution fusion | flops 687470592 | bytes 22880260 | tf_op jit(solution)/shard_map/while/body/eval_jaxpr/rgke,gse->gkrs/dot_general | solution.py:64
  214.9 5.2 %fusion.94 = f32[4,512]{1,0:T(4,128)S(1)} fusion(f32[2560,512,4]{1,0,2:T(8,128)S(1)} %get-tuple-element.155, f32[4,512]{1,0:T(4,128)S(1)} %get-tuple-element.156, pred[512,2560]{0,1:T(8,128)(4,1)S(1)} %pad_add_fusion.2), kind=kLoop, calls=%fused_computation.3.clone.1 | loop fusion | flops 26212352 | bytes 22298624 | tf_op jit(solution)/shard_map/while/body/eval_jaxpr/reduce_sum | solution.py:78
  220.2 5.9 %fusion.96 = bf16[512,1,4,64]{0,3,2,1:T(8,128)(2,1)S(1)} fusion(f32[2560,512,4]{1,0,2:T(8,128)S(1)} %get-tuple-element.155, f32[4,512]{1,0:T(4,128)S(1)} %get-tuple-element.156, pred[512,2560]{0,1:T(8,128)(4,1)S(1)} %pad_add_fusion.2, bf16[1,512,64]{1,2,0:T(8,128)(2,1)S(1)} %get-tuple-element.157, bf16[1,2048,64]{1,2,0:T(8,128)(2,1)S(1)} %copy.39, ...), kind=kOutput, calls=%fused_computation.17.clone.1 | convolution fusion | flops 698220544 | bytes 22888448 | tf_op jit(solution)/shard_map/while/body/eval_jaxpr/gkrs,gse->rgke/dot_general | solution.py:81
  230.1 4.7 %convolution_convert_fusion = bf16[1024,2048]{1,0:T(8,128)(2,1)} fusion(bf16[256,2048]{1,0:T(8,128)(2,1)} %param.25, bf16[1536,256]{0,1:T(8,128)(2,1)} %get-tuple-element.47), kind=kOutput, calls=%fused_computation.39 | convolution fusion | flops 1075838976 | bytes 5767168 | tf_op jit(solution)/shard_map/dot_general | solution.py:167
  234.8 48.7 %reduce-scatter.3.cloned.1.call-done = bf16[128,2048]{1,0:T(8,128)(2,1)} async-done(((bf16[1024,2048]{1,0:T(8,128)(2,1)}), bf16[128,2048]{1,0:T(8,128)(2,1)}) %reduce-scatter.3.cloned.1.call-update) | async-done | bytes 524304 | tf_op jit(solution)/shard_map/reduce_scatter | solution.py:166
  287.0 44.2 %all-gather.8.cloned.1.call-done = bf16[512,2048]{1,0:T(8,128)(2,1)} async-done(((bf16[128,2048]{1,0:T(8,128)(2,1)}), bf16[512,2048]{1,0:T(8,128)(2,1)}) %all-gather.8.cloned.1.call-update) | async-done | bytes 2097168 | tf_op jit(solution)/shard_map/all_gather | solution.py:174
  331.1 6.5 %fusion.73 = f32[512,1024]{1,0:T(8,128)} fusion(bf16[512,2048]{1,0:T(8,128)(2,1)} %all-gather.8.cloned.1.call-done, bf16[2048,1024]{1,0:T(8,128)(2,1)} %param.27), kind=kOutput, calls=%fused_computation.120 | convolution fusion | flops 2147483648 | bytes 8388608 | tf_op jit(solution)/shard_map/dot_general | solution.py:175
  337.6 10.6 %convolution_convert_fusion.1 = bf16[512,2048]{1,0:T(8,128)(2,1)} fusion(bf16[1024,2048]{1,0:T(8,128)(2,1)} %param.29, f32[512,1024]{1,0:T(8,128)} %fusion.73, bf16[512,2048]{1,0:T(8,128)(2,1)} %all-gather.8.cloned.1.call-done, bf16[2048,1024]{1,0:T(8,128)(2,1)} %param.28), kind=kOutput, calls=%fused_computation.40 | convolution fusion | flops 4299161600 | bytes 14680064 | tf_op jit(solution)/shard_map/dot_general | solution.py:179
  348.3 42.2 %reduce-scatter.5.cloned.1.call-done = bf16[128,2048]{1,0:T(8,128)(2,1)} async-done(((bf16[512,2048]{1,0:T(8,128)(2,1)}), bf16[128,2048]{1,0:T(8,128)(2,1)}) %reduce-scatter.5.cloned.1.call-update) | async-done | bytes 524304 | tf_op jit(solution)/shard_map/reduce_scatter | solution.py:178
  392.0 21.5 %psum.14 = bf16[4,2048]{1,0:T(4,128)(2,1)S(1)} all-reduce(bf16[4,2048]{1,0:T(4,128)(2,1)S(1)} %convolution_convert_fusion.2), channel_id=1, replica_groups=mesh['req'=4,'tok'=8] {'tok'}, use_global_device_ids=true, to_apply=%region_11.12 | all-reduce | flops 8192 | bytes 32768 | tf_op jit(solution)/shard_map/psum | solution.py:188
  414.1 10.3 %fusion.72 = (f32[4]{0:T(128)S(1)}, f32[4,4000]{1,0:T(4,128)S(1)}) fusion(bf16[4000,2048]{1,0:T(8,128)(2,1)} %param.31, bf16[4,2048]{1,0:T(4,128)(2,1)S(1)} %psum.14, f32[2048]{0:T(1024)S(1)} %convert_element_type.108, f32[4]{0:T(128)S(1)} %get-tuple-element.92), kind=kOutput, calls=%fused_computation.119 | convolution fusion | flops 65584764 | bytes 16472608 | tf_op jit(solution)/shard_map/dot_general | solution.py:194
  424.4 14.4 %pmax.7 = f32[4]{0:T(128)S(1)} all-reduce(f32[4]{0:T(128)S(1)} %get-tuple-element.96), channel_id=1, replica_groups=mesh['req'=4,'tok'=8] {'tok'}, use_global_device_ids=true, to_apply=%region_14.15 | all-reduce | flops 4 | bytes 32 | tf_op jit(solution)/shard_map/pmax | solution.py:197
  439.7 11.8 %psum.15 = f32[4]{0:T(128)S(1)} all-reduce(f32[4]{0:T(128)S(1)} %exponential_reduce_fusion), channel_id=1, replica_groups=mesh['req'=4,'tok'=8] {'tok'}, use_global_device_ids=true, to_apply=%region_16.17 | all-reduce | flops 4 | bytes 32 | tf_op jit(solution)/shard_map/psum | solution.py:198
  (178 shorter events, 64.9 us)
Async XLA Ops:
  7.2 43.6 %copy-start = (bf16[4,2048,128]{2,1,0:T(8,128)(2,1)S(1)}, bf16[4,2048,128]{2,1,0:T(8,128)(2,1)}, u32[]{:S(2)}) copy-start(bf16[4,2048,128]{2,1,0:T(8,128)(2,1)} %param.24) | copy-start | bytes 6291460
  7.2 31.3 %all-gather.4.cloned.1.call-start = ((), (), s32[]{:S(2)}) async-start(), calls=%async_computation.3 | async-start | bytes 1310720 | tf_op jit(solution)/shard_map/all_gather | solution.py:134
  7.9 83.8 %all-gather.6.cloned.1.call-start = ((), (), s32[]{:S(2)}) async-start(), calls=%async_computation.4 | async-start | bytes 4718592 | tf_op jit(solution)/shard_map/all_gather | solution.py:121
  40.0 7.6 %copy-start.17 = (s32[4]{0:T(128)S(1)}, s32[4]{0:T(128)}, u32[]{:S(2)}) copy-start(s32[4]{0:T(128)} %param.20) | copy-start | bytes 52
  40.0 7.6 %copy-start.18 = (s32[1,4]{1,0:T(1,128)S(1)}, s32[1,4]{1,0:T(1,128)}, u32[]{:S(2)}) copy-start(s32[1,4]{1,0:T(1,128)} %param.19) | copy-start | bytes 52
  41.6 34.0 %all-to-all-start = ((bf16[4,8,256,128]{2,3,0,1:T(8,128)(2,1)}), bf16[4,8,256,128]{2,3,0,1:T(8,128)(2,1)}, u32[]{:S(2)}, u32[]{:S(2)}) async-start(bf16[4,8,256,128]{2,3,0,1:T(8,128)(2,1)} %bitcast.128), calls=%async_computation | async-start | bytes 4194304 | tf_op jit(solution)/shard_map/all_to_all | solution.py:136
  46.7 236.8 %reduce-scatter.3.cloned.1.call-start = ((), (), s32[]{:S(2)}) async-start(), calls=%async_computation.5 | async-start | bytes 4718592 | tf_op jit(solution)/shard_map/reduce_scatter | solution.py:166
  102.2 8.0 %copy-start.11 = (pred[512]{0:T(512)(128)(4,1)}, pred[512]{0:T(512)(128)(4,1)S(1)}, u32[]{:S(2)}) copy-start(pred[512]{0:T(512)(128)(4,1)S(1)} %iota_compare_fusion.9) | copy-start | bytes 1540 | tf_op jit(solution)/shard_map/while
  111.5 1.0 copy-start.10
  117.2 5.2 %copy-start.12 = (pred[512]{0:T(512)(128)(4,1)S(1)}, pred[512]{0:T(512)(128)(4,1)}, u32[]{:S(2)}) copy-start(pred[512]{0:T(512)(128)(4,1)} %copy-done.11) | copy-start | bytes 1540 | tf_op jit(solution)/shard_map/while
  122.4 5.9 %copy-start.3 = (bf16[1536,256]{0,1:T(8,128)(2,1)S(1)}, bf16[1536,256]{0,1:T(8,128)(2,1)}, u32[]{:S(2)}) copy-start(bf16[1536,256]{0,1:T(8,128)(2,1)} %get-tuple-element.173) | copy-start | bytes 2359300 | tf_op jit(solution)/shard_map/while
  134.4 8.0 %copy-start.11 = (pred[512]{0:T(512)(128)(4,1)}, pred[512]{0:T(512)(128)(4,1)S(1)}, u32[]{:S(2)}) copy-start(pred[512]{0:T(512)(128)(4,1)S(1)} %iota_compare_fusion.9) | copy-start | bytes 1540 | tf_op jit(solution)/shard_map/while
  149.3 5.2 %copy-start.12 = (pred[512]{0:T(512)(128)(4,1)S(1)}, pred[512]{0:T(512)(128)(4,1)}, u32[]{:S(2)}) copy-start(pred[512]{0:T(512)(128)(4,1)} %copy-done.11) | copy-start | bytes 1540 | tf_op jit(solution)/shard_map/while
  154.6 5.9 %copy-start.3 = (bf16[1536,256]{0,1:T(8,128)(2,1)S(1)}, bf16[1536,256]{0,1:T(8,128)(2,1)}, u32[]{:S(2)}) copy-start(bf16[1536,256]{0,1:T(8,128)(2,1)} %get-tuple-element.173) | copy-start | bytes 2359300 | tf_op jit(solution)/shard_map/while
  167.2 8.0 %copy-start.11 = (pred[512]{0:T(512)(128)(4,1)}, pred[512]{0:T(512)(128)(4,1)S(1)}, u32[]{:S(2)}) copy-start(pred[512]{0:T(512)(128)(4,1)S(1)} %iota_compare_fusion.9) | copy-start | bytes 1540 | tf_op jit(solution)/shard_map/while
  176.5 1.0 copy-start.10
  182.1 5.2 %copy-start.12 = (pred[512]{0:T(512)(128)(4,1)S(1)}, pred[512]{0:T(512)(128)(4,1)}, u32[]{:S(2)}) copy-start(pred[512]{0:T(512)(128)(4,1)} %copy-done.11) | copy-start | bytes 1540 | tf_op jit(solution)/shard_map/while
  187.4 5.9 %copy-start.3 = (bf16[1536,256]{0,1:T(8,128)(2,1)S(1)}, bf16[1536,256]{0,1:T(8,128)(2,1)}, u32[]{:S(2)}) copy-start(bf16[1536,256]{0,1:T(8,128)(2,1)} %get-tuple-element.173) | copy-start | bytes 2359300 | tf_op jit(solution)/shard_map/while
  200.0 8.0 %copy-start.11 = (pred[512]{0:T(512)(128)(4,1)}, pred[512]{0:T(512)(128)(4,1)S(1)}, u32[]{:S(2)}) copy-start(pred[512]{0:T(512)(128)(4,1)S(1)} %iota_compare_fusion.9) | copy-start | bytes 1540 | tf_op jit(solution)/shard_map/while
  214.9 5.2 %copy-start.12 = (pred[512]{0:T(512)(128)(4,1)S(1)}, pred[512]{0:T(512)(128)(4,1)}, u32[]{:S(2)}) copy-start(pred[512]{0:T(512)(128)(4,1)} %copy-done.11) | copy-start | bytes 1540 | tf_op jit(solution)/shard_map/while
  220.2 5.9 %copy-start.3 = (bf16[1536,256]{0,1:T(8,128)(2,1)S(1)}, bf16[1536,256]{0,1:T(8,128)(2,1)}, u32[]{:S(2)}) copy-start(bf16[1536,256]{0,1:T(8,128)(2,1)} %get-tuple-element.173) | copy-start | bytes 2359300 | tf_op jit(solution)/shard_map/while
  230.0 4.7 %copy-start.13 = (bf16[2048]{0:T(1024)(128)(2,1)S(1)}, bf16[2048]{0:T(1024)(128)(2,1)}, u32[]{:S(2)}) copy-start(bf16[2048]{0:T(1024)(128)(2,1)} %param.26) | copy-start | bytes 12292
  230.0 53.5 %copy-start.2 = (bf16[128,2048]{1,0:T(8,128)(2,1)S(1)}, bf16[128,2048]{1,0:T(8,128)(2,1)}, u32[]{:S(2)}) copy-start(bf16[128,2048]{1,0:T(8,128)(2,1)} %param.17) | copy-start | bytes 1572868
  234.7 96.4 %all-gather.8.cloned.1.call-start = ((), (), s32[]{:S(2)}) async-start(), calls=%async_computation.6 | async-start | bytes 2621440 | tf_op jit(solution)/shard_map/all_gather | solution.py:174
  286.9 103.6 %reduce-scatter.5.cloned.1.call-start = ((), (), s32[]{:S(2)}) async-start(), calls=%async_computation.7 | async-start | bytes 2621440 | tf_op jit(solution)/shard_map/reduce_scatter | solution.py:178
  337.6 10.7 %copy-start.14 = (bf16[2048]{0:T(1024)(128)(2,1)S(1)}, bf16[2048]{0:T(1024)(128)(2,1)}, u32[]{:S(2)}) copy-start(bf16[2048]{0:T(1024)(128)(2,1)} %param.30) | copy-start | bytes 12292
  337.6 52.9 %copy-start.6 = (bf16[128,2048]{1,0:T(8,128)(2,1)S(1)}, bf16[128,2048]{1,0:T(8,128)(2,1)}, u32[]{:S(2)}) copy-start(bf16[128,2048]{1,0:T(8,128)(2,1)} %reduce-scatter.3.cloned.1.call-done) | copy-start | bytes 1572868
  348.2 43.5 %copy-start.15 = (s32[4]{0:T(128)S(1)}, s32[4]{0:T(128)}, u32[]{:S(2)}) copy-start(s32[4]{0:T(128)} %get-tuple-element.94) | copy-start | bytes 52
  391.8 32.7 %copy-start.7 = (bf16[128,2048]{1,0:T(8,128)(2,1)}, bf16[128,2048]{1,0:T(8,128)(2,1)S(1)}, u32[]{:S(2)}) copy-start(bf16[128,2048]{1,0:T(8,128)(2,1)S(1)} %fusion.45) | copy-start | bytes 1572868
  414.1 24.9 %copy-start.9 = (bf16[1024,1,128]{0,2,1:T(8,128)(2,1)S(1)}, bf16[1024,1,128]{0,2,1:T(8,128)(2,1)}, u32[]{:S(2)}) copy-start(bf16[1024,1,128]{0,2,1:T(8,128)(2,1)} %copy-done.8) | copy-start | bytes 786436
  414.1 37.9 %copy-start.1 = (bf16[4,2048,128]{2,1,0:T(8,128)(2,1)S(1)}, bf16[4,2048,128]{2,1,0:T(8,128)(2,1)}, u32[]{:S(2)}) copy-start(bf16[4,2048,128]{2,1,0:T(8,128)(2,1)} %param.24) | copy-start | bytes 6291460
  438.8 13.2 %copy-start.16 = (f32[4]{0:T(128)}, f32[4]{0:T(128)S(1)}, u32[]{:S(2)}) copy-start(f32[4]{0:T(128)S(1)} %pmax.7) | copy-start | bytes 52
  (11 other events, 10.0 us)
Sparse Core Ops, SparseCore 0:
  9.6 28.8 all-gather.3
  40.9 50.7 all-gather.5
  234.9 48.6 reduce-scatter.2
  287.0 44.0 all-gather.7
  348.4 42.0 reduce-scatter.4
where the time goes:
time: 464 us; the launch traced here: 459 us
  waiting for transfers between devices  200 us (43%)
  matrix products  79 us (17%)
  local copies, waits for them, and re-layouts  50.7 us (11%)
  blocking collectives  47.6 us (10%)
  other arithmetic  45.6 us (10%)
  loops' own time  16.2 us (3%)
  between operations  14 us (3%)
  starting transfers between devices  5.27 us (1%)
    reduce_scatter x1, waiting for transfers between devices, shards(): lax.psum_scatter(jnp.dot(attended, out_weight, preferred_element_type=jnp...  48.7 us
    all_gather x1, waiting for transfers between devices, shards(): shard_part = lax.all_gather(mlp_in, 'req', axis=0, tiled=True)  44.2 us
    reduce_scatter x1, waiting for transfers between devices, shards(): lax.psum_scatter(jnp.dot(hidden_act, down_weight, preferred_element_type=...  42.2 us
    all_gather x1, waiting for transfers between devices, shards(): every_owner = lax.all_gather(prefix_cache, 'req', axis=0, tiled=True)  26.5 us
    all_to_all x1, waiting for transfers between devices, shards(): lax.all_to_all(routed, 'tok', split_axis=1, concat_axis=2, tiled=True)  24.8 us
    dot_general x4, matrix products, request_attention(): jnp.einsum('gkrs,gse->rgke', rounded, value_rows, preferred_element_type=...  23.7 us
    psum x1, blocking collectives, shards(): last_rows = lax.psum(picked.astype(jnp.bfloat16), 'tok').astype(jnp.float32)  21.5 us
    reduce_sum x4, other arithmetic, request_attention(): totals = jnp.sum(weights, axis=-1, keepdims=True)  20.8 us
  transfers between devices with their start and end apart: 6, of which 6 were waited for; matrix products, arithmetic and copies ran while one was open for 3% of the time, Pallas kernels for 0%

commit v1 on v0

v1 whole, which is shorter than its diff:
```python
import math

import jax
import jax.numpy as jnp
from jax import lax
from jax.experimental import pallas as pl
from jax.experimental.pallas import tpu as pltpu
from jax.sharding import PartitionSpec as P

HD = 64
PRE_LEN = 16384


epsilon = 1e-05
neg_large = -1e30


def rms_scale(values, gain_vec):
    widened = values.astype(jnp.float32)
    mean_square = jnp.mean(widened * widened, axis=-1, keepdims=True)
    return widened * lax.rsqrt(mean_square + epsilon) * gain_vec.astype(jnp.float32)


def owner_layout(lengths, row_count):
    end_rows = jnp.cumsum(lengths)
    starts = end_rows - lengths
    row_index = jnp.arange(row_count)
    member = (row_index[:, None] >= starts[None, :]) & (row_index[:, None] < end_rows[None, :])
    offsets = row_index - jnp.sum(jnp.where(member, starts[None, :], 0), axis=1)
    return (starts, end_rows, offsets)


def slot_lookup(chosen, prefix_slot):
    table_index = jnp.arange(prefix_slot.shape[0])
    hits = chosen[:, None] == table_index[None, :]
    return jnp.sum(jnp.where(hits, prefix_slot[None, :], 0), axis=1)


def attention_kernel(
    member_count,
    heads,
    piece,
    most_rows,
    window_len,
    chunk,
    suffix_chunk,
    scalars,
    q_ref,
    cos_ref,
    sin_ref,
    *refs,
):
    windows = refs[:member_count]
    suffix_ref, out_ref, query_scr, high_scr, total_scr, acc_scr, result_scr = refs[member_count:]
    requests = 4
    rows = q_ref.shape[1]
    half = HD // 2
    width = heads * rows
    member = scalars[3 * requests]
    tile = pl.program_id(0)
    first_row = (tile * member_count + member) * rows
    cosine = cos_ref[...]
    sine = sin_ref[...]
    for head in range(heads):
        low = q_ref[head * HD : head * HD + half, :]
        high = q_ref[head * HD + half : (head + 1) * HD, :]
        cols = pl.ds(head * rows, rows)
        turned = jnp.concatenate(
            [
                low * cosine - high * sine,
                high * cosine + low * sine,
                jnp.zeros((HD, rows), jnp.float32),
            ],
            axis=0,
        )
        query_scr[:, cols] = (turned * (HD**-0.5 * math.log2(math.e))).astype(jnp.bfloat16)

    def absorb(keyvals, row_of_key, visible_fn):
        scores = jnp.dot(keyvals, query_scr[...], preferred_element_type=jnp.float32)
        if visible_fn is not None:
            scores = jnp.where(visible_fn(scores.shape), scores, neg_large)
        before = high_scr[...]
        after = jnp.maximum(before, jnp.max(scores, axis=0, keepdims=True))
        weights = jnp.exp2(scores - after)
        fade = jnp.exp2(before - after)
        total_scr[...] = total_scr[...] * fade + jnp.sum(weights, axis=0, keepdims=True)
        mixed = lax.dot_general(
            keyvals,
            weights.astype(jnp.bfloat16),
            (((0,), (0,)), ((), ())),
            preferred_element_type=jnp.float32,
        )
        acc_scr[...] = acc_scr[...] * fade + mixed[HD:, :]
        high_scr[...] = after

    lane_row = first_row + lax.broadcasted_iota(jnp.int32, (1, width), 1) % rows

    def one_request(request, carry):
        start = scalars[request]
        end = scalars[requests + request]
        slot = scalars[2 * requests + request]

        @pl.when((start < first_row + rows) & (end > first_row))
        def _():
            high_scr[...] = jnp.full(high_scr.shape, neg_large, jnp.float32)
            total_scr[...] = jnp.zeros(total_scr.shape, jnp.float32)
            acc_scr[...] = jnp.zeros(acc_scr.shape, jnp.float32)
            offset = lane_row - start
            local_len = windows[0].shape[1]
            for first in reversed(range(0, local_len, chunk)):
                for shift in range(member_count):
                    part = lax.rem(member + shift, member_count)

                    def prefix_seen(shape, first=first, part=part):
                        index = first + lax.broadcasted_iota(jnp.int32, (shape[0], 1), 0)
                        position = (index // piece * member_count + part) * piece + index % piece
                        return position > offset

                    masked = first // piece * member_count * piece < most_rows
                    absorb(
                        windows[shift][slot, first : first + chunk, :],
                        None,
                        prefix_seen if masked else None,
                    )

            def suffix_step(step, inner):
                base = pl.multiple_of(step * suffix_chunk, suffix_chunk)

                def suffix_seen(shape):
                    key_row = base + lax.broadcasted_iota(jnp.int32, (shape[0], 1), 0)
                    return (
                        (key_row >= start)
                        & (key_row <= lane_row)
                        & (lane_row - key_row < window_len)
                    )

                absorb(suffix_ref[pl.ds(base, suffix_chunk), :], None, suffix_seen)
                return inner

            lax.fori_loop(
                start // suffix_chunk,
                (jnp.minimum(first_row + rows, end) - 1) // suffix_chunk + 1,
                suffix_step,
                0,
            )
            mine = (lane_row >= start) & (lane_row < end)
            result_scr[...] = jnp.where(mine, acc_scr[...] / total_scr[...], result_scr[...])

        return carry

    lax.fori_loop(0, requests, one_request, 0)
    for head in range(heads):
        out_ref[head * HD : (head + 1) * HD, :] = result_scr[
            :, head * rows : (head + 1) * rows
        ].astype(jnp.bfloat16)


def attention(scalars, queries, cosine, sine, windows, suffix, rows, piece, most_rows, window_len):
    width, own = queries.shape
    heads = width // HD
    member_count = len(windows)
    chunk = min(512, windows[0].shape[1])
    suffix_chunk = 256

    def whole(array):
        return pl.BlockSpec(array.shape, lambda t, s, n=array.ndim: (0,) * n)

    return pl.pallas_call(
        lambda *refs: attention_kernel(
            member_count, heads, piece, most_rows, window_len, chunk, suffix_chunk, *refs
        ),
        out_shape=jax.ShapeDtypeStruct((width, own), jnp.bfloat16),
        grid_spec=pltpu.PrefetchScalarGridSpec(
            num_scalar_prefetch=1,
            grid=(own // rows,),
            in_specs=[
                pl.BlockSpec((width, rows), lambda t, s: (0, t)),
                pl.BlockSpec((HD // 2, rows), lambda t, s: (0, t)),
                pl.BlockSpec((HD // 2, rows), lambda t, s: (0, t)),
                *[whole(window) for window in windows],
                whole(suffix),
            ],
            out_specs=pl.BlockSpec((width, rows), lambda t, s: (0, t)),
            scratch_shapes=[
                pltpu.VMEM((2 * HD, heads * rows), jnp.bfloat16),
                pltpu.VMEM((1, heads * rows), jnp.float32),
                pltpu.VMEM((1, heads * rows), jnp.float32),
                pltpu.VMEM((HD, heads * rows), jnp.float32),
                pltpu.VMEM((HD, heads * rows), jnp.float32),
            ],
        ),
        compiler_params=pltpu.CompilerParams(vmem_limit_bytes=48 * 2**20),
        cost_estimate=pl.CostEstimate(
            flops=20_000_000_000, bytes_accessed=8_000_000, transcendentals=10_000_000
        ),
        name="attention",
    )(scalars, queries, cosine, sine, *windows, suffix)


def shards(
    hidden_in,
    suffix_len,
    prefix_of,
    prefix_slot,
    prefix_cache,
    attn_gain,
    query_weight,
    keyval_weight,
    out_weight,
    mlp_gain,
    gate_weight,
    up_weight,
    down_weight,
    final_gain,
    head_weight,
):
    tok_count = lax.axis_size("tok")
    tok_place = lax.axis_index("tok")
    tok_rows = hidden_in.shape[0]
    own_rows = tok_rows * tok_count
    most_rows = own_rows // 2
    kv_count = keyval_weight.shape[0]
    members = tok_count // kv_count
    kv_head = tok_place // members
    member = tok_place % members
    alike = [[h * members + g for h in range(kv_count)] for g in range(members)]

    def shifted(array, shift):
        pairs = [
            (h * members + (g + shift) % members, h * members + g)
            for h in range(kv_count)
            for g in range(members)
        ]
        return lax.ppermute(array, "tok", pairs)

    lengths = suffix_len[0]
    starts, end_rows, offsets = owner_layout(lengths, own_rows)
    query_parts = [query_weight] + [shifted(query_weight, s) for s in range(1, members)]
    out_parts = [out_weight] + [shifted(out_weight, s) for s in range(1, members)]
    normed = rms_scale(hidden_in, attn_gain).astype(jnp.bfloat16)
    rows_here = lax.all_gather(normed, "tok", axis=0, tiled=True, axis_index_groups=alike)
    window_block = prefix_cache.shape[2]
    piece = window_block // members
    dealt = prefix_cache.reshape(1, tok_count, piece, 2 * HD)
    dealt = lax.all_to_all(dealt, "tok", split_axis=1, concat_axis=2, tiled=True)[:, 0]
    windows = [lax.all_gather(dealt, "req", axis=0, tiled=True)]
    windows += [shifted(windows[0], s) for s in range(1, members)]
    positions = lax.dynamic_index_in_dim(
        offsets.reshape(kv_count, members, tok_rows), member, 1, keepdims=False
    ).reshape(-1)
    positions = positions + PRE_LEN
    half = HD // 2
    levels = jnp.arange(half).astype(jnp.float32)
    inverse = jnp.exp(levels * (-2.0 * math.log(10000.0) / HD))
    angles = inverse[:, None] * positions.astype(jnp.float32)[None, :]
    cosine, sine = jnp.cos(angles), jnp.sin(angles)
    kv_weight = lax.dynamic_index_in_dim(keyval_weight, kv_head, 0, keepdims=False)
    keyvals = jnp.dot(rows_here, kv_weight, preferred_element_type=jnp.float32)
    low, high = keyvals[:, :half], keyvals[:, half:HD]
    cos_rows, sin_rows = cosine.T, sine.T
    keyvals = jnp.concatenate(
        [
            low * cos_rows - high * sin_rows,
            high * cos_rows + low * sin_rows,
            keyvals[:, HD:],
        ],
        axis=-1,
    ).astype(jnp.bfloat16)
    suffix = jnp.zeros((members, kv_count, tok_rows, 2 * HD), jnp.bfloat16)
    for s in range(members):
        part = keyvals if s == 0 else shifted(keyvals, s)
        suffix = lax.dynamic_update_index_in_dim(
            suffix, part.reshape(kv_count, tok_rows, 2 * HD), (member + s) % members, 0
        )
    suffix = jnp.transpose(suffix, (1, 0, 2, 3)).reshape(own_rows, 2 * HD)
    cache_width = kv_count * 2 * HD // tok_count
    cache_offset = tok_place * cache_width % (2 * HD)
    suffix_cache = lax.dynamic_slice_in_dim(suffix, cache_offset, cache_width, 1)
    queries = lax.dot_general(
        jnp.concatenate(query_parts, axis=1),
        rows_here,
        (((0,), (1,)), ((), ())),
        preferred_element_type=jnp.float32,
    )
    cache_rows = slot_lookup(prefix_of[0], prefix_slot)
    scalars = jnp.concatenate([starts, end_rows, cache_rows, member[None]]).astype(jnp.int32)
    attended = attention(
        scalars,
        queries,
        cosine,
        sine,
        windows,
        suffix,
        tok_rows,
        piece,
        most_rows,
        window_block * tok_count,
    )
    projected_back = lax.psum_scatter(
        lax.dot_general(
            attended,
            jnp.concatenate(out_parts, axis=0),
            (((0,), (0,)), ((), ())),
            preferred_element_type=jnp.float32,
        ).astype(jnp.bfloat16),
        "tok",
        scatter_dimension=0,
        tiled=True,
        axis_index_groups=alike,
    ).astype(jnp.float32)
    middle = (hidden_in.astype(jnp.float32) + projected_back).astype(jnp.bfloat16)
    mlp_in = rms_scale(middle, mlp_gain).astype(jnp.bfloat16)
    shard_part = lax.all_gather(mlp_in, "req", axis=0, tiled=True)
    gate_proj = jnp.dot(shard_part, gate_weight, preferred_element_type=jnp.float32)
    lifted = jnp.dot(shard_part, up_weight, preferred_element_type=jnp.float32)
    hidden_act = (jax.nn.silu(gate_proj) * lifted).astype(jnp.bfloat16)
    summed = lax.psum_scatter(
        jnp.dot(hidden_act, down_weight, preferred_element_type=jnp.float32).astype(jnp.bfloat16),
        "req",
        scatter_dimension=0,
        tiled=True,
    ).astype(jnp.float32)
    final_state = (middle.astype(jnp.float32) + summed).astype(jnp.bfloat16)
    local_index = jnp.arange(tok_rows) + tok_place * tok_rows
    picker = (local_index[None, :] == (end_rows - 1)[:, None]).astype(jnp.bfloat16)
    picked = jnp.dot(picker, final_state, preferred_element_type=jnp.float32)
    last_rows = lax.psum(picked.astype(jnp.bfloat16), "tok").astype(jnp.float32)
    mean_square = jnp.mean(last_rows * last_rows, axis=-1, keepdims=True)
    spread = jnp.sqrt(mean_square + epsilon)
    final_normed = (
        last_rows * lax.rsqrt(mean_square + epsilon) * final_gain.astype(jnp.float32)
    ).astype(jnp.bfloat16)
    logits = lax.dot_general(
        final_normed, head_weight, (((1,), (1,)), ((), ())), preferred_element_type=jnp.float32
    )
    local_high = jnp.max(logits, axis=-1)
    local_sum = jnp.sum(jnp.exp(logits - local_high[:, None]), axis=-1)
    pairs = lax.all_gather(jnp.stack([local_high, local_sum]), "tok", axis=0)
    highest = jnp.max(pairs[:, 0], axis=0)
    summed_exp = jnp.sum(pairs[:, 1] * jnp.exp(pairs[:, 0] - highest[None, :]), axis=0)
    log_total = highest + jnp.log(summed_exp)
    return (final_state, suffix_cache, spread[:, 0][None, :], highest[None, :], log_total[None, :])


def solution(mesh):
    placed = (
        P(("req", "tok"), None),
        P("req", None),
        P("req", None),
        P(),
        P("req", None, "tok", None),
        P(),
        P(None, "tok"),
        P(),
        P("tok", None),
        P(),
        P(None, "req"),
        P(None, "req"),
        P("req", None),
        P(),
        P("tok", None),
    )
    return jax.shard_map(
        shards,
        mesh=mesh,
        in_specs=placed,
        out_specs=(
            P(("req", "tok"), None),
            P("req", "tok"),
            P("req", None),
            P("req", None),
            P("req", None),
        ),
        check_vma=False,
    )
```

time: 464 us -> 337 us (0.73); the launches traced: 459 us -> 336 us
  matrix products: 79 us -> 38 us
  local copies, waits for them, and re-layouts: 50.7 us -> 10.9 us
  Pallas kernels: 0 us -> 33.7 us
  other arithmetic: 45.6 us -> 13.3 us
  waiting for transfers between devices: 200 us -> 180 us
  loops' own time: 16.2 us -> 0 us
  blocking collectives: 47.6 us -> 42.9 us
    dot_general x10 -> x3, matrix products: 51.4 us -> 10.6 us  [the longest x1 4.17 us: shards(): lax.dot_general(attended, jnp.concatenate(out_parts, axis=0), (((0,), (0,...]
    pallas_call x0 -> x1, Pallas kernels: none -> 33.7 us  [attention(): pl.pallas_call(lambda *refs: attention_kernel(member_count, heads, piece,...]
    all_to_all x1 -> x0, waiting for transfers between devices: 24.8 us -> none  [shards(): lax.all_to_all(routed, 'tok', split_axis=1, concat_axis=2, tiled=True)]
    reduce_sum x5 -> x2, other arithmetic: 21 us -> 0.42 us  [the longest x1 0.23 us: shards(): local_sum = jnp.sum(jnp.exp(logits - local_high[:, None]), axis=-1)]
    all_gather x2, waiting for transfers between devices: 39.6 us -> 58 us  [the longest x1 36.7 us: shards(): lax.all_gather(normed, 'tok', axis=0, tiled=True, axis_index_groups=alike)]
    another operation x1 -> x0, loops' own time: 16.2 us -> none  [shards(): lax.scan(one_request, buffer, (starts, lengths, cache_rows))]
    dynamic_slice x13 -> x1, local copies, waits for them, and re-layouts: 15.4 us -> 0.84 us  [shards(): lax.dynamic_slice_in_dim(suffix, cache_offset, cache_width, 1)]
    pmax x1 -> x0, blocking collectives: 14.4 us -> none  [shards(): highest = lax.pmax(jnp.max(logits, axis=-1), 'tok')]
  transfers between devices with their start and end apart: 6 -> 9, of which waited for: 6 -> 5; matrix products, arithmetic and copies ran while one was open for 3% -> 6% of each run, Pallas kernels for 0% -> 10%
where the time goes in v1:
time: 337 us; the launch traced here: 336 us
  waiting for transfers between devices  180 us (53%)
  blocking collectives  42.9 us (13%)
  matrix products  38 us (11%)
  Pallas kernels  33.7 us (10%)
  between operations  14 us (4%)
  other arithmetic  13.3 us (4%)
  local copies, waits for them, and re-layouts  10.9 us (3%)
  starting transfers between devices  3.45 us (1%)
    all_gather x1, waiting for transfers between devices, shards(): shard_part = lax.all_gather(mlp_in, 'req', axis=0, tiled=True)  44 us
    reduce_scatter x1, waiting for transfers between devices, shards(): lax.psum_scatter(jnp.dot(hidden_act, down_weight, preferred_element_type=...  39 us
    reduce_scatter x1, waiting for transfers between devices, shards(): lax.psum_scatter(lax.dot_general(attended, jnp.concatenate(out_parts, axi...  38.8 us
    all_gather x1, waiting for transfers between devices, shards(): lax.all_gather(normed, 'tok', axis=0, tiled=True, axis_index_groups=alike)  36.7 us
    pallas_call x1, Pallas kernels, attention(): pl.pallas_call(lambda *refs: attention_kernel(member_count, heads, piece,...  33.7 us
    psum x1, blocking collectives, shards(): last_rows = lax.psum(picked.astype(jnp.bfloat16), 'tok').astype(jnp.float32)  21.5 us
    all_gather x1, waiting for transfers between devices, shards(): windows = [lax.all_gather(dealt, 'req', axis=0, tiled=True)]  21.4 us
    all_gather x1, blocking collectives, shards(): pairs = lax.all_gather(jnp.stack([local_high, local_sum]), 'tok', axis=0)  11 us
  transfers between devices with their start and end apart: 9, of which 5 were waited for; matrix products, arithmetic and copies ran while one was open for 6% of the time, Pallas kernels for 10%

profile of v1, /device:TPU:9, one launch (start us, length us, event | category | flops | bytes accessed | tf_op | source)
XLA Modules:
  0.0 336.2 jit_solution(1114982826004972194)
XLA Ops:
  7.3 10.4 %all_to_all.4 = bf16[1,8,128,128]{3,2,0,1:T(8,128)(2,1)} all-to-all(bf16[1,8,128,128]{3,2,0,1:T(8,128)(2,1)} %bitcast.65), channel_id=1, replica_groups=mesh['req'=4,'tok'=8] {'tok'}, dimensions={1} | all-to-all | bytes 524288 | tf_op jit(solution)/shard_map/all_to_all | solution.py:245
  18.5 1.2 fusion.7
  19.7 2.0 fusion.9
  21.8 1.4 collective-permute-start
  24.2 21.4 %all-gather.8.cloned.1.call-done.refs_4_ = bf16[4,1024,128]{2,1,0:T(8,128)(2,1)} async-done(((bf16[1,1024,128]{2,1,0:T(8,128)(2,1)}), bf16[4,1024,128]{2,1,0:T(8,128)(2,1)}) %all-gather.8.cloned.1.call-update) | async-done | bytes 1048592 | tf_op jit(solution)/shard_map/all_gather | solution.py:246
  45.5 0.9 collective-permute-start.1
  46.5 36.7 %all-gather.6.cloned.1.call-done = bf16[512,2048]{1,0:T(8,128)(2,1)} async-done(((bf16[128,2048]{1,0:T(8,128)(2,1)}), bf16[512,2048]{1,0:T(8,128)(2,1)}) %all-gather.6.cloned.1.call-update) | async-done | bytes 2097168 | tf_op jit(solution)/shard_map/all_gather | solution.py:241
  83.1 2.6 fusion.15
  87.4 3.8 %fusion.refs_1_ = f32[512,512]{1,0:T(8,128)} fusion(bf16[512,2048]{1,0:T(8,128)(2,1)S(1)} %copy-done.5, bf16[2048,256]{1,0:T(8,128)(2,1)} %collective-permute-done, bf16[2048,256]{1,0:T(8,128)(2,1)} %param.21), kind=kOutput, calls=%fused_computation.3 | convolution fusion | flops 1077936128 | bytes 5242880 | tf_op jit(solution)/shard_map/dot_general | solution.py:279
  91.2 0.8 copy.43
  92.0 0.7 copy.41
  92.7 0.8 copy.42
  93.5 1.2 maximum_dynamic-update-slice_fusion
  94.8 1.7 copy.44
  96.4 0.9 constant_dynamic-update-slice_fusion
  97.4 1.2 copy-done.2
  98.6 33.7 %attention.1 = bf16[512,512]{1,0:T(8,128)(2,1)S(1)} custom-call(s32[13]{0:T(128)S(1)} %pad_add_fusion.refs_0_, f32[512,512]{1,0:T(8,128)S(1)} %copy-done.2, f32[32,512]{1,0:T(8,128)S(1)} %get-tuple-element.26.refs_2_, f32[32,512]{1,0:T(8,128)S(1)} %get-tuple-element.25.refs_3_, bf16[4,1024,128]{2,1,0:T(8,128)(2,1)S(1)} %copy-done.1, ...), custom_call_target="tpu_custom_call" | custom-call | flops 20000000000 | bytes 8000000 | tf_op jit(solution)/shard_map/attention/pallas_call | solution.py:168
  132.4 4.2 %convolution_convert_fusion.1 = bf16[512,2048]{1,0:T(8,128)(2,1)} fusion(bf16[512,512]{1,0:T(8,128)(2,1)S(1)} %attention.1, bf16[256,2048]{1,0:T(8,128)(2,1)} %collective-permute-done.3, bf16[256,2048]{1,0:T(8,128)(2,1)} %param.23), kind=kOutput, calls=%fused_computation.1 | convolution fusion | flops 1078984704 | bytes 4718592 | tf_op jit(solution)/shard_map/dot_general | solution.py:300
  137.2 38.8 %reduce-scatter.3.cloned.1.call-done = bf16[128,2048]{1,0:T(8,128)(2,1)} async-done(((bf16[512,2048]{1,0:T(8,128)(2,1)}), bf16[128,2048]{1,0:T(8,128)(2,1)}) %reduce-scatter.3.cloned.1.call-update) | async-done | bytes 524304 | tf_op jit(solution)/shard_map/reduce_scatter | solution.py:299
  176.0 1.3 fusion.11
  177.3 2.0 fusion.13
  179.6 44.0 %all-gather.10.cloned.1.call-done = bf16[512,2048]{1,0:T(8,128)(2,1)} async-done(((bf16[128,2048]{1,0:T(8,128)(2,1)}), bf16[512,2048]{1,0:T(8,128)(2,1)}) %all-gather.10.cloned.1.call-update) | async-done | bytes 2097168 | tf_op jit(solution)/shard_map/all_gather | solution.py:313
  223.6 6.5 %fusion.51 = f32[512,1024]{1,0:T(8,128)} fusion(bf16[512,2048]{1,0:T(8,128)(2,1)} %all-gather.10.cloned.1.call-done, bf16[2048,1024]{1,0:T(8,128)(2,1)} %param.25), kind=kOutput, calls=%fused_computation.95 | convolution fusion | flops 2147483648 | bytes 8388608 | tf_op jit(solution)/shard_map/dot_general | solution.py:314
  230.1 10.6 %convolution_convert_fusion = bf16[512,2048]{1,0:T(8,128)(2,1)} fusion(bf16[1024,2048]{1,0:T(8,128)(2,1)} %param.27, f32[512,1024]{1,0:T(8,128)} %fusion.51, bf16[512,2048]{1,0:T(8,128)(2,1)} %all-gather.10.cloned.1.call-done, bf16[2048,1024]{1,0:T(8,128)(2,1)} %param.26), kind=kOutput, calls=%fused_computation | convolution fusion | flops 4299161600 | bytes 14680064 | tf_op jit(solution)/shard_map/dot_general | solution.py:318
  241.4 0.8 constant_dynamic-slice_fusion
  242.3 1.7 copy.40
  244.0 39.0 %reduce-scatter.5.cloned.1.call-done = bf16[128,2048]{1,0:T(8,128)(2,1)} async-done(((bf16[512,2048]{1,0:T(8,128)(2,1)}), bf16[128,2048]{1,0:T(8,128)(2,1)}) %reduce-scatter.5.cloned.1.call-update) | async-done | bytes 524304 | tf_op jit(solution)/shard_map/reduce_scatter | solution.py:317
  283.0 1.3 fusion.14
  284.3 0.8 copy-done.6
  285.3 21.5 %psum.7 = bf16[4,2048]{1,0:T(4,128)(2,1)S(1)} all-reduce(bf16[4,2048]{1,0:T(4,128)(2,1)S(1)} %convolution_convert_fusion.2), channel_id=1, replica_groups=mesh['req'=4,'tok'=8] {'tok'}, use_global_device_ids=true, to_apply=%region_7.8 | all-reduce | flops 8192 | bytes 32768 | tf_op jit(solution)/shard_map/psum | solution.py:327
  307.4 10.1 %fusion.50 = (f32[4]{0:T(128)S(1)}, f32[4,4000]{1,0:T(4,128)S(1)}) fusion(bf16[4000,2048]{1,0:T(8,128)(2,1)} %param.29, bf16[4,2048]{1,0:T(4,128)(2,1)S(1)} %psum.7, f32[2048]{0:T(1024)S(1)} %convert_element_type.99, f32[4]{0:T(128)S(1)} %get-tuple-element.27), kind=kOutput, calls=%fused_computation.94 | convolution fusion | flops 65584764 | bytes 16472608 | tf_op jit(solution)/shard_map/dot_general | solution.py:333
  317.8 11.0 %all-gather.1 = f32[8,2,4]{2,1,0:T(2,128)S(1)} all-gather(f32[1,2,4]{2,1,0:T(2,128)S(1)} %maximum_bitcast_fusion), channel_id=2, replica_groups=mesh['req'=4,'tok'=8] {'tok'}, dimensions={0}, use_global_device_ids=true | all-gather | bytes 288 | tf_op jit(solution)/shard_map/all_gather | solution.py:338
  (69 shorter events, 7.2 us)
Async XLA Ops:
  7.2 76.0 %copy-start = (bf16[4,2048,128]{2,1,0:T(8,128)(2,1)S(1)}, bf16[4,2048,128]{2,1,0:T(8,128)(2,1)}, u32[]{:S(2)}) copy-start(bf16[4,2048,128]{2,1,0:T(8,128)(2,1)} %param.22) | copy-start | bytes 6291460
  7.2 16.1 %copy-start.10 = (s32[1,4]{1,0:T(1,128)S(1)}, s32[1,4]{1,0:T(1,128)}, u32[]{:S(2)}) copy-start(s32[1,4]{1,0:T(1,128)} %param.16) | copy-start | bytes 52
  7.2 16.3 %copy-start.11 = (s32[4]{0:T(128)S(1)}, s32[4]{0:T(128)}, u32[]{:S(2)}) copy-start(s32[4]{0:T(128)} %param.18) | copy-start | bytes 52
  7.2 16.3 %copy-start.12 = (s32[1,4]{1,0:T(1,128)S(1)}, s32[1,4]{1,0:T(1,128)}, u32[]{:S(2)}) copy-start(s32[1,4]{1,0:T(1,128)} %param.17) | copy-start | bytes 52
  7.2 38.3 %all-gather.8.cloned.1.call-start = ((), (), s32[]{:S(2)}) async-start(), calls=%async_computation.4 | async-start | bytes 1310720 | tf_op jit(solution)/shard_map/all_gather | solution.py:246
  17.7 65.4 %all-gather.6.cloned.1.call-start = ((), (), s32[]{:S(2)}) async-start(), calls=%async_computation.3 | async-start | bytes 2621440 | tf_op jit(solution)/shard_map/all_gather | solution.py:241
  21.8 154.3 %reduce-scatter.3.cloned.1.call-start = ((), (), s32[]{:S(2)}) async-start(), calls=%async_computation.5 | async-start | bytes 2621440 | tf_op jit(solution)/shard_map/reduce_scatter | solution.py:299
  21.8 65.6 %collective-permute-start = (bf16[2048,256]{1,0:T(8,128)(2,1)}, bf16[2048,256]{1,0:T(8,128)(2,1)}, u32[]{:S(2)}, u32[]{:S(2)}) collective-permute-start(bf16[2048,256]{1,0:T(8,128)(2,1)} %param.21), channel_id=1, source_target_pairs={{1,0},{0,1},{3,2},{2,3},{5,4},{4,5},{7,6},{6,7},{9,8},{8,9},{11,10... | collective-permute-start | bytes 3145736 | tf_op jit(solution)/shard_map/ppermute | solution.py:234
  23.2 109.1 %collective-permute-start.3 = (bf16[256,2048]{1,0:T(8,128)(2,1)}, bf16[256,2048]{1,0:T(8,128)(2,1)}, u32[]{:S(2)}, u32[]{:S(2)}) collective-permute-start(bf16[256,2048]{1,0:T(8,128)(2,1)} %param.23), channel_id=1, source_target_pairs={{1,0},{0,1},{3,2},{2,3},{5,4},{4,5},{7,6},{6,7},{9,8},{8,9},{11,10... | collective-permute-start | bytes 3145736 | tf_op jit(solution)/shard_map/ppermute | solution.py:234
  45.5 51.8 %collective-permute-start.1 = (bf16[4,1024,128]{2,1,0:T(8,128)(2,1)}, bf16[4,1024,128]{2,1,0:T(8,128)(2,1)}, u32[]{:S(2)}, u32[]{:S(2)}) collective-permute-start(bf16[4,1024,128]{2,1,0:T(8,128)(2,1)} %all-gather.8.cloned.1.call-done.refs_4_), channel_id=1, source_target_pairs={{1,0},{0,1},{3,2},{2,3},{5,4},{4,5},{7,6},{6,7},{9,8},{8,9},{11,10... | collective-permute-start | bytes 3145736 | tf_op jit(solution)/shard_map/ppermute | solution.py:234
  83.1 4.3 %copy-start.5 = (bf16[512,2048]{1,0:T(8,128)(2,1)S(1)}, bf16[512,2048]{1,0:T(8,128)(2,1)}, u32[]{:S(2)}) copy-start(bf16[512,2048]{1,0:T(8,128)(2,1)} %all-gather.6.cloned.1.call-done) | copy-start | bytes 6291460
  86.7 10.7 %copy-start.1 = (bf16[4,1024,128]{2,1,0:T(8,128)(2,1)S(1)}, bf16[4,1024,128]{2,1,0:T(8,128)(2,1)}, u32[]{:S(2)}) copy-start(bf16[4,1024,128]{2,1,0:T(8,128)(2,1)} %all-gather.8.cloned.1.call-done.refs_4_) | copy-start | bytes 3145732
  86.7 8.0 %collective-permute-start.2 = (bf16[512,128]{0,1:T(8,128)(2,1)}, bf16[512,128]{0,1:T(8,128)(2,1)}, u32[]{:S(2)}, u32[]{:S(2)}) collective-permute-start(bf16[512,128]{0,1:T(8,128)(2,1)} %pad_maximum_fusion), channel_id=1, source_target_pairs={{1,0},{0,1},{3,2},{2,3},{5,4},{4,5},{7,6},{6,7},{9,8},{8,9},{11,10... | collective-permute-start | bytes 393224 | tf_op jit(solution)/shard_map/ppermute | solution.py:234
  97.4 1.2 copy-start.2
  136.5 0.7 copy-start.7
  136.5 39.5 %copy-start.3 = (bf16[128,2048]{1,0:T(8,128)(2,1)S(1)}, bf16[128,2048]{1,0:T(8,128)(2,1)}, u32[]{:S(2)}) copy-start(bf16[128,2048]{1,0:T(8,128)(2,1)} %param.15) | copy-start | bytes 1572868
  136.6 87.1 %all-gather.10.cloned.1.call-start = ((), (), s32[]{:S(2)}) async-start(), calls=%async_computation.6 | async-start | bytes 2621440 | tf_op jit(solution)/shard_map/all_gather | solution.py:313
  179.4 103.6 %reduce-scatter.5.cloned.1.call-start = ((), (), s32[]{:S(2)}) async-start(), calls=%async_computation.7 | async-start | bytes 2621440 | tf_op jit(solution)/shard_map/reduce_scatter | solution.py:317
  240.7 0.7 copy-start.8
  240.8 42.2 %copy-start.4 = (bf16[128,2048]{1,0:T(8,128)(2,1)S(1)}, bf16[128,2048]{1,0:T(8,128)(2,1)}, u32[]{:S(2)}) copy-start(bf16[128,2048]{1,0:T(8,128)(2,1)} %reduce-scatter.3.cloned.1.call-done) | copy-start | bytes 1572868
  284.3 0.8 copy-start.6
  328.8 0.9 copy-start.9
Sparse Core Ops, SparseCore 0:
  17.9 27.6 all-gather.7
  48.0 35.1 all-gather.5
  136.7 39.3 reduce-scatter.2
  179.5 44.0 all-gather.9
  240.9 42.0 reduce-scatter.4

commit v2 on v1

--- a/solution.py
+++ b/solution.py
@@ -197,6 +197,177 @@
     )(scalars, queries, cosine, sine, *windows, suffix)
 
 
+MESH = pl.DeviceIdType.MESH
+
+
+def enter(groups):
+    barrier = pltpu.get_barrier_semaphore()
+    signals = 0
+    for axis, count, stride in groups:
+        place = lax.axis_index(axis)
+        for shift in range(1, count):
+            peer = lax.rem(place // stride + shift, count) * stride + lax.rem(place, stride)
+            pl.semaphore_signal(barrier, inc=1, device_id={axis: peer}, device_id_type=MESH)
+            signals += 1
+    pl.semaphore_wait(barrier, signals)
+
+
+def start_exchange(item, source, target, send, recv, local, row):
+    scatter, (axis, count, stride) = item
+    place = lax.axis_index(axis)
+    mine = place // stride
+    own = pltpu.make_async_copy(
+        source.at[mine] if scatter else source, target.at[mine], local.at[row]
+    )
+    own.start()
+    copies = [own]
+    for shift in range(1, count):
+        peer = lax.rem(mine + shift, count)
+        copy = pltpu.make_async_remote_copy(
+            src_ref=source.at[peer] if scatter else source,
+            dst_ref=target.at[mine],
+            send_sem=send.at[row, shift],
+            recv_sem=recv.at[row, shift],
+            device_id={axis: peer * stride + lax.rem(place, stride)},
+            device_id_type=MESH,
+        )
+        copy.start()
+        copies.append(copy)
+    return copies
+
+
+def remote_call(body, inputs, outputs, rows, most, collective_id, name):
+    return pl.pallas_call(
+        body,
+        out_shape=outputs,
+        in_specs=[pl.BlockSpec(memory_space=pl.ANY)] * len(inputs),
+        out_specs=jax.tree.map(lambda _: pl.BlockSpec(memory_space=pl.ANY), outputs),
+        scratch_shapes=[
+            pltpu.SemaphoreType.DMA((rows, most)),
+            pltpu.SemaphoreType.DMA((rows, most)),
+            pltpu.SemaphoreType.DMA((rows,)),
+        ],
+        compiler_params=pltpu.CompilerParams(collective_id=collective_id, has_side_effects=True),
+        name=name,
+    )(*inputs)
+
+
+def exchange(array, scatter, group, collective_id, name):
+    def body(source, target, send, recv, local):
+        enter([group])
+        for copy in start_exchange((scatter, group), source, target, send, recv, local, 0):
+            copy.wait()
+
+    shape = array.shape if scatter else (group[1],) + array.shape
+    return remote_call(
+        body, [array], jax.ShapeDtypeStruct(shape, array.dtype), 1, group[1], collective_id, name
+    )
+
+
+def front_exchange(normed, dealt, alike, everyone, owners):
+    def body(rows_ref, dealt_ref, all_rows, taken, windows, send, recv, local):
+        enter([everyone, owners])
+        first = start_exchange((True, everyone), dealt_ref, taken, send, recv, local, 0)
+        second = start_exchange((False, alike), rows_ref, all_rows, send, recv, local, 1)
+        for copy in first:
+            copy.wait()
+        third = start_exchange((False, owners), taken, windows, send, recv, local, 2)
+        for copy in second + third:
+            copy.wait()
+
+    outputs = [
+        jax.ShapeDtypeStruct((alike[1],) + normed.shape, normed.dtype),
+        jax.ShapeDtypeStruct(dealt.shape, dealt.dtype),
+        jax.ShapeDtypeStruct((owners[1],) + dealt.shape, dealt.dtype),
+    ]
+    most = max(alike[1], everyone[1], owners[1])
+    return remote_call(body, [normed, dealt], outputs, 3, most, 0, "front_exchange")
+
+
+def relay_gather(block, axis, count, collective_id, name):
+    def body(source, target, send, recv, local):
+        place = lax.axis_index(axis)
+        has_left, has_right = place > 0, place < count - 1
+        barrier = pltpu.get_barrier_semaphore()
+
+        @pl.when(has_left)
+        def _():
+            pl.semaphore_signal(barrier, inc=1, device_id={axis: place - 1}, device_id_type=MESH)
+
+        @pl.when(has_right)
+        def _():
+            pl.semaphore_signal(barrier, inc=1, device_id={axis: place + 1}, device_id_type=MESH)
+
+        @pl.when(has_left & has_right)
+        def _():
+            pl.semaphore_wait(barrier, 2)
+
+        @pl.when(jnp.logical_not(has_left & has_right))
+        def _():
+            pl.semaphore_wait(barrier, 1)
+
+        own = pltpu.make_async_copy(source, target.at[place], local.at[0])
+        own.start()
+
+        def hop(step, toward):
+            owner = lax.rem(place - toward * step + count, count)
+            row = (1 - toward) // 2
+            return pltpu.make_async_remote_copy(
+                src_ref=source if step == 0 else target.at[owner],
+                dst_ref=target.at[owner],
+                send_sem=send.at[row, step],
+                recv_sem=recv.at[row, step],
+                device_id={axis: lax.rem(place + toward + count, count)},
+                device_id_type=MESH,
+            )
+
+        def sends(step, toward):
+            if toward == 1:
+                return has_right & (place - step >= 0)
+            return has_left & (place + step <= count - 1)
+
+        def arrives(step, toward):
+            if toward == 1:
+                return place - 1 - step >= 0
+            return place + 1 + step <= count - 1
+
+        for step in range(count - 1):
+            for toward in (1, -1):
+                if step > 0:
+
+                    @pl.when(arrives(step - 1, toward))
+                    def _():
+                        hop(step - 1, toward).wait_recv()
+
+                @pl.when(sends(step, toward))
+                def _():
+                    hop(step, toward).start()
+
+        for toward in (1, -1):
+
+            @pl.when(arrives(count - 2, toward))
+            def _():
+                hop(count - 2, toward).wait_recv()
+
+            for step in range(count - 1):
+
+                @pl.when(sends(step, toward))
+                def _():
+                    hop(step, toward).wait_send()
+
+        own.wait()
+
+    return remote_call(
+        body,
+        [block],
+        jax.ShapeDtypeStruct((count,) + block.shape, block.dtype),
+        2,
+        count,
+        collective_id,
+        name,
+    )
+
+
 def shards(
     hidden_in,
     suffix_len,
@@ -223,7 +394,10 @@
     members = tok_count // kv_count
     kv_head = tok_place // members
     member = tok_place % members
-    alike = [[h * members + g for h in range(kv_count)] for g in range(members)]
+    owner_count = lax.axis_size("req")
+    alike = ("tok", kv_count, members)
+    everyone = ("tok", tok_count, 1)
+    owners = ("req", owner_count, 1)
 
     def shifted(array, shift):
         pairs = [
@@ -238,12 +412,12 @@
     query_parts = [query_weight] + [shifted(query_weight, s) for s in range(1, members)]
     out_parts = [out_weight] + [shifted(out_weight, s) for s in range(1, members)]
     normed = rms_scale(hidden_in, attn_gain).astype(jnp.bfloat16)
-    rows_here = lax.all_gather(normed, "tok", axis=0, tiled=True, axis_index_groups=alike)
     window_block = prefix_cache.shape[2]
     piece = window_block // members
-    dealt = prefix_cache.reshape(1, tok_count, piece, 2 * HD)
-    dealt = lax.all_to_all(dealt, "tok", split_axis=1, concat_axis=2, tiled=True)[:, 0]
-    windows = [lax.all_gather(dealt, "req", axis=0, tiled=True)]
+    dealt = prefix_cache.reshape(tok_count, piece, 2 * HD)
+    rows_here, unused, windows = front_exchange(normed, dealt, alike, everyone, owners)
+    rows_here = rows_here.reshape(kv_count * tok_rows, -1)
+    windows = [windows.reshape(owner_count, tok_count * piece, 2 * HD)]
     windows += [shifted(windows[0], s) for s in range(1, members)]
     positions = lax.dynamic_index_in_dim(
         offsets.reshape(kv_count, members, tok_rows), member, 1, keepdims=False
@@ -296,21 +470,18 @@
         most_rows,
         window_block * tok_count,
     )
-    projected_back = lax.psum_scatter(
-        lax.dot_general(
-            attended,
-            jnp.concatenate(out_parts, axis=0),
-            (((0,), (0,)), ((), ())),
-            preferred_element_type=jnp.float32,
-        ).astype(jnp.bfloat16),
-        "tok",
-        scatter_dimension=0,
-        tiled=True,
-        axis_index_groups=alike,
-    ).astype(jnp.float32)
+    partial = lax.dot_general(
+        attended,
+        jnp.concatenate(out_parts, axis=0),
+        (((0,), (0,)), ((), ())),
+        preferred_element_type=jnp.float32,
+    ).astype(jnp.bfloat16)
+    partial = exchange(partial.reshape(kv_count, tok_rows, -1), True, alike, 1, "out_exchange")
+    projected_back = jnp.sum(partial.astype(jnp.float32), axis=0)
     middle = (hidden_in.astype(jnp.float32) + projected_back).astype(jnp.bfloat16)
     mlp_in = rms_scale(middle, mlp_gain).astype(jnp.bfloat16)
-    shard_part = lax.all_gather(mlp_in, "req", axis=0, tiled=True)
+    shard_part = relay_gather(mlp_in, "req", owner_count, 2, "mlp_gather")
+    shard_part = shard_part.reshape(owner_count * tok_rows, -1)
     gate_proj = jnp.dot(shard_part, gate_weight, preferred_element_type=jnp.float32)
     lifted = jnp.dot(shard_part, up_weight, preferred_element_type=jnp.float32)
     hidden_act = (jax.nn.silu(gate_proj) * lifted).astype(jnp.bfloat16)
@@ -324,7 +495,8 @@
     local_index = jnp.arange(tok_rows) + tok_place * tok_rows
     picker = (local_index[None, :] == (end_rows - 1)[:, None]).astype(jnp.bfloat16)
     picked = jnp.dot(picker, final_state, preferred_element_type=jnp.float32)
-    last_rows = lax.psum(picked.astype(jnp.bfloat16), "tok").astype(jnp.float32)
+    picked = exchange(picked.astype(jnp.bfloat16), False, everyone, 3, "last_exchange")
+    last_rows = jnp.sum(picked.astype(jnp.float32), axis=0)
     mean_square = jnp.mean(last_rows * last_rows, axis=-1, keepdims=True)
     spread = jnp.sqrt(mean_square + epsilon)
     final_normed = (
@@ -335,7 +507,8 @@
     )
     local_high = jnp.max(logits, axis=-1)
     local_sum = jnp.sum(jnp.exp(logits - local_high[:, None]), axis=-1)
-    pairs = lax.all_gather(jnp.stack([local_high, local_sum]), "tok", axis=0)
+    pairs = jnp.pad(jnp.stack([local_high, local_sum]), ((0, 6), (0, 128 - starts.shape[0])))
+    pairs = exchange(pairs, False, everyone, 4, "tail_exchange")[:, :, : starts.shape[0]]
     highest = jnp.max(pairs[:, 0], axis=0)
     summed_exp = jnp.sum(pairs[:, 1] * jnp.exp(pairs[:, 0] - highest[None, :]), axis=0)
     log_total = highest + jnp.log(summed_exp)

time: 337 us -> 260 us (0.77); the launches traced: 336 us -> 255 us
  waiting for transfers between devices: 180 us -> 40.3 us
  Pallas kernels: 33.7 us -> 138 us
  blocking collectives: 42.9 us -> 0 us
  local copies, waits for them, and re-layouts: 10.9 us -> 6.71 us
  other arithmetic: 13.3 us -> 16.9 us
    pallas_call x0 -> x5, Pallas kernels: none -> 110 us  [remote_call(): pl.pallas_call(body, out_shape=outputs, in_specs=[pl.BlockSpec(memory_spa...]
    all_gather x3 -> x0, waiting for transfers between devices: 102 us -> none  [the longest x1 44 us: shards(): shard_part = lax.all_gather(mlp_in, 'req', axis=0, tiled=True)]
    reduce_scatter x1 -> x0, waiting for transfers between devices: 38.8 us -> none  [shards(): lax.psum_scatter(lax.dot_general(attended, jnp.concatenate(out_parts, axi...]
    psum x1 -> x0, blocking collectives: 21.5 us -> none  [shards(): last_rows = lax.psum(picked.astype(jnp.bfloat16), 'tok').astype(jnp.float32)]
    all_gather x1 -> x0, blocking collectives: 11 us -> none  [shards(): pairs = lax.all_gather(jnp.stack([local_high, local_sum]), 'tok', axis=0)]
    all_to_all x1 -> x0, blocking collectives: 10.4 us -> none  [shards(): lax.all_to_all(dealt, 'tok', split_axis=1, concat_axis=2, tiled=True)[:, 0]]
    pallas_call x1, Pallas kernels: 33.7 us -> 27.5 us  [attention(): pl.pallas_call(lambda *refs: attention_kernel(member_count, heads, piece,...]
    unnamed x27 -> x23, local copies, waits for them, and re-layouts: 5.03 us -> 1.49 us
  transfers between devices with their start and end apart: 9 -> 5, of which waited for: 5 -> 1; matrix products, arithmetic and copies ran while one was open for 6% -> 8% of each run, Pallas kernels for 10% -> 24%
where the time goes in v2:
time: 260 us; the launch traced here: 255 us
  Pallas kernels  138 us (53%)
  waiting for transfers between devices  40.3 us (15%)
  matrix products  38 us (15%)
  other arithmetic  16.9 us (6%)
  between operations  14.3 us (6%)
  local copies, waits for them, and re-layouts  6.71 us (3%)
    pallas_call x5, Pallas kernels, remote_call(): pl.pallas_call(body, out_shape=outputs, in_specs=[pl.BlockSpec(memory_spa...  110 us
    reduce_scatter x1, waiting for transfers between devices, shards(): lax.psum_scatter(jnp.dot(hidden_act, down_weight, preferred_element_type=...  40.3 us
    pallas_call x1, Pallas kernels, attention(): pl.pallas_call(lambda *refs: attention_kernel(member_count, heads, piece,...  27.5 us
    dot_general x1, matrix products, shards(): jnp.dot(hidden_act, down_weight, preferred_element_type=jnp.float32)  10.6 us
    dot_general x1, matrix products, shards(): lax.dot_general(final_normed, head_weight, (((1,), (1,)), ((), ())), pref...  10.1 us
    dot_general x1, matrix products, shards(): jnp.dot(shard_part, gate_weight, preferred_element_type=jnp.float32)  6.49 us
  transfers between devices with their start and end apart: 5, of which 1 were waited for; matrix products, arithmetic and copies ran while one was open for 8% of the time, Pallas kernels for 24%

profile of v2, /device:TPU:9, one launch (start us, length us, event | category | flops | bytes accessed | tf_op | source)
XLA Modules:
  0.0 255.4 jit_solution(7554177874052708370)
XLA Ops:
  7.2 0.7 collective-permute-start
  8.1 0.8 reduce-window.4
  8.9 0.7 fusion.40
  9.5 1.2 fusion.7
  10.8 0.7 convert_element_type.84
  11.6 2.0 fusion.9.rows_ref
  13.6 33.2 %front_exchange.1 = (bf16[4,128,2048]{2,1,0:T(8,128)(2,1)}, bf16[8,128,128]{2,1,0:T(8,128)(2,1)}, bf16[4,8,128,128]{3,2,1,0:T(8,128)(2,1)}) custom-call(bf16[128,2048]{1,0:T(8,128)(2,1)} %fusion.9.rows_ref, bf16[8,128,128]{2,1,0:T(8,128)(2,1)} %bitcast.72), custom_call_target="tpu_custom_call" | custom-call | tf_op jit(solution)/shard_map/front_exchange/pallas_call | solution.py:240
  46.9 2.5 fusion.15
  51.5 0.8 copy.36
  52.2 0.8 copy.34
  53.0 0.8 copy.35
  53.8 1.2 maximum_dynamic-update-slice_fusion
  55.0 1.7 copy.37
  56.7 0.9 constant_dynamic-update-slice_fusion
  57.6 3.5 %fusion.refs_1_ = f32[512,512]{1,0:T(8,128)S(1)} fusion(bf16[512,2048]{1,0:T(8,128)(2,1)} %bitcast.66, bf16[2048,256]{1,0:T(8,128)(2,1)} %collective-permute-done, bf16[2048,256]{1,0:T(8,128)(2,1)} %param.21), kind=kOutput, calls=%fused_computation.4 | convolution fusion | flops 1077936128 | bytes 5242880 | tf_op jit(solution)/shard_map/dot_general | solution.py:453
  61.2 27.5 %attention.1 = bf16[512,512]{1,0:T(8,128)(2,1)S(1)} custom-call(s32[13]{0:T(128)S(1)} %pad_add_fusion.refs_0_, f32[512,512]{1,0:T(8,128)S(1)} %fusion.refs_1_, f32[32,512]{1,0:T(8,128)S(1)} %get-tuple-element.27.refs_2_, f32[32,512]{1,0:T(8,128)S(1)} %get-tuple-element.26.refs_3_, bf16[4,1024,128]{2,1,0:T(8,128)(2,1)S(1)} %bitcast.62, ...), custom_call_target="tpu_custom_call" | custom-call | flops 20000000000 | bytes 8000000 | tf_op jit(solution)/shard_map/attention/pallas_call | solution.py:168
  88.7 3.9 %convolution_convert_fusion.1 = bf16[512,2048]{1,0:T(8,128)(2,1)} fusion(bf16[512,512]{1,0:T(8,128)(2,1)S(1)} %attention.1, bf16[256,2048]{1,0:T(8,128)(2,1)} %collective-permute-done.3, bf16[256,2048]{1,0:T(8,128)(2,1)S(1)} %copy-done.8), kind=kOutput, calls=%fused_computation.2 | convolution fusion | flops 1078984704 | bytes 4718592 | tf_op jit(solution)/shard_map/dot_general | solution.py:473
  92.6 26.5 %out_exchange.1 = bf16[4,128,2048]{2,1,0:T(8,128)(2,1)} custom-call(bf16[4,128,2048]{2,1,0:T(8,128)(2,1)} %bitcast.67), custom_call_target="tpu_custom_call" | custom-call | tf_op jit(solution)/shard_map/out_exchange/pallas_call | solution.py:240
  119.1 2.1 convert_reduce_fusion
  121.6 1.0 fusion.13.source
  122.6 39.3 %mlp_gather.1 = bf16[4,128,2048]{2,1,0:T(8,128)(2,1)} custom-call(bf16[128,2048]{1,0:T(8,128)(2,1)} %fusion.13.source), custom_call_target="tpu_custom_call" | custom-call | tf_op jit(solution)/shard_map/mlp_gather/pallas_call | solution.py:240
  161.8 6.5 %fusion.48 = f32[512,1024]{1,0:T(8,128)} fusion(bf16[512,2048]{1,0:T(8,128)(2,1)} %bitcast.63, bf16[2048,1024]{1,0:T(8,128)(2,1)} %param.25), kind=kOutput, calls=%fused_computation.96 | convolution fusion | flops 2147483648 | bytes 8388608 | tf_op jit(solution)/shard_map/dot_general | solution.py:485
  168.3 10.6 %convolution_convert_fusion = bf16[512,2048]{1,0:T(8,128)(2,1)} fusion(bf16[1024,2048]{1,0:T(8,128)(2,1)} %param.27, f32[512,1024]{1,0:T(8,128)} %fusion.48, bf16[512,2048]{1,0:T(8,128)(2,1)} %bitcast.64, bf16[2048,1024]{1,0:T(8,128)(2,1)} %param.26), kind=kOutput, calls=%fused_computation.1 | convolution fusion | flops 4299161600 | bytes 14680064 | tf_op jit(solution)/shard_map/dot_general | solution.py:489
  179.8 0.8 copy.33
  180.6 40.3 %reduce-scatter.2.cloned.1.call-done = bf16[128,2048]{1,0:T(8,128)(2,1)} async-done(((bf16[512,2048]{1,0:T(8,128)(2,1)}), bf16[128,2048]{1,0:T(8,128)(2,1)}) %reduce-scatter.2.cloned.1.call-update) | async-done | bytes 524304 | tf_op jit(solution)/shard_map/reduce_scatter | solution.py:488
  220.9 1.2 fusion.14
  222.1 0.8 convolution_convert_fusion.2.source
  222.9 6.1 %last_exchange.1 = bf16[8,4,2048]{2,1,0:T(4,128)(2,1)} custom-call(bf16[4,2048]{1,0:T(4,128)(2,1)} %convolution_convert_fusion.2.source), custom_call_target="tpu_custom_call" | custom-call | tf_op jit(solution)/shard_map/last_exchange/pallas_call | solution.py:240
  229.0 1.0 convert_reduce_fusion.1
  230.6 10.1 %fusion.47 = (f32[4]{0:T(128)S(1)}, f32[4,4000]{1,0:T(4,128)S(1)}) fusion(bf16[4000,2048]{1,0:T(8,128)(2,1)} %param.29, f32[4,2048]{1,0:T(4,128)S(1)} %convert_reduce_fusion.1, f32[2048]{0:T(1024)S(1)} %convert_element_type.101, f32[4]{0:T(128)S(1)} %get-tuple-element.28), kind=kOutput, calls=%fused_computation.95 | convolution fusion | flops 65576572 | bytes 16488992 | tf_op jit(solution)/shard_map/dot_general | solution.py:505
  241.6 5.2 %tail_exchange.1 = f32[8,8,128]{2,1,0:T(8,128)} custom-call(f32[8,128]{1,0:T(8,128)} %select_maximum_fusion.source), custom_call_target="tpu_custom_call" | custom-call | tf_op jit(solution)/shard_map/tail_exchange/pallas_call | solution.py:240
  246.8 0.9 fusion.46
  (57 shorter events, 5.8 us)
Async XLA Ops:
  7.2 39.7 %copy-start = (bf16[4,2048,128]{2,1,0:T(8,128)(2,1)S(1)}, bf16[4,2048,128]{2,1,0:T(8,128)(2,1)}, u32[]{:S(2)}) copy-start(bf16[4,2048,128]{2,1,0:T(8,128)(2,1)} %param.22) | copy-start | bytes 6291460
  7.2 213.7 %reduce-scatter.2.cloned.1.call-start = ((), (), s32[]{:S(2)}) async-start(), calls=%async_computation.1 | async-start | bytes 2621440 | tf_op jit(solution)/shard_map/reduce_scatter | solution.py:488
  7.2 50.4 %collective-permute-start = (bf16[2048,256]{1,0:T(8,128)(2,1)}, bf16[2048,256]{1,0:T(8,128)(2,1)}, u32[]{:S(2)}, u32[]{:S(2)}) collective-permute-start(bf16[2048,256]{1,0:T(8,128)(2,1)} %param.21), channel_id=1, source_target_pairs={{1,0},{0,1},{3,2},{2,3},{5,4},{4,5},{7,6},{6,7},{9,8},{8,9},{11,10... | collective-permute-start | bytes 3145736 | tf_op jit(solution)/shard_map/ppermute | solution.py:408
  8.0 80.7 %collective-permute-start.3 = (bf16[256,2048]{1,0:T(8,128)(2,1)}, bf16[256,2048]{1,0:T(8,128)(2,1)}, u32[]{:S(2)}, u32[]{:S(2)}) collective-permute-start(bf16[256,2048]{1,0:T(8,128)(2,1)} %param.23), channel_id=1, source_target_pairs={{1,0},{0,1},{3,2},{2,3},{5,4},{4,5},{7,6},{6,7},{9,8},{8,9},{11,10... | collective-permute-start | bytes 3145736 | tf_op jit(solution)/shard_map/ppermute | solution.py:408
  13.6 37.3 %copy-start.7 = (s32[1,4]{1,0:T(1,128)S(1)}, s32[1,4]{1,0:T(1,128)}, u32[]{:S(2)}) copy-start(s32[1,4]{1,0:T(1,128)} %param.16) | copy-start | bytes 52
  13.6 37.3 %copy-start.9 = (s32[4]{0:T(128)S(1)}, s32[4]{0:T(128)}, u32[]{:S(2)}) copy-start(s32[4]{0:T(128)} %param.18) | copy-start | bytes 52
  13.6 37.3 %copy-start.10 = (s32[1,4]{1,0:T(1,128)S(1)}, s32[1,4]{1,0:T(1,128)}, u32[]{:S(2)}) copy-start(s32[1,4]{1,0:T(1,128)} %param.17) | copy-start | bytes 52
  46.8 3.6 %copy-start.1 = (bf16[4,8,128,128]{3,2,1,0:T(8,128)(2,1)S(1)}, bf16[4,8,128,128]{3,2,1,0:T(8,128)(2,1)}, u32[]{:S(2)}) copy-start(bf16[4,8,128,128]{3,2,1,0:T(8,128)(2,1)} %get-tuple-element.8) | copy-start | bytes 3145732
  46.8 6.9 %copy-start.4 = (bf16[2048]{0:T(1024)(128)(2,1)S(1)}, bf16[2048]{0:T(1024)(128)(2,1)}, u32[]{:S(2)}) copy-start(bf16[2048]{0:T(1024)(128)(2,1)} %param.24) | copy-start | bytes 12292
  50.4 4.7 %collective-permute-start.2 = (bf16[512,128]{0,1:T(8,128)(2,1)}, bf16[512,128]{0,1:T(8,128)(2,1)}, u32[]{:S(2)}, u32[]{:S(2)}) collective-permute-start(bf16[512,128]{0,1:T(8,128)(2,1)} %pad_maximum_fusion), channel_id=1, source_target_pairs={{1,0},{0,1},{3,2},{2,3},{5,4},{4,5},{7,6},{6,7},{9,8},{8,9},{11,10... | collective-permute-start | bytes 393224 | tf_op jit(solution)/shard_map/ppermute | solution.py:408
  50.4 10.7 %collective-permute-start.1 = (bf16[4,1024,128]{2,1,0:T(8,128)(2,1)S(1)}, bf16[4,1024,128]{2,1,0:T(8,128)(2,1)}, u32[]{:S(2)}, u32[]{:S(2)}) collective-permute-start(bf16[4,1024,128]{2,1,0:T(8,128)(2,1)S(1)} %bitcast.61), channel_id=1, source_target_pairs={{1,0},{0,1},{3,2},{2,3},{5,4},{4,5},{7,6},{6,7},{9,8},{8,9},{11,10... | collective-permute-start | bytes 3145736 | tf_op jit(solution)/shard_map/ppermute | solution.py:408
  61.2 27.5 %copy-start.8 = (bf16[256,2048]{1,0:T(8,128)(2,1)S(1)}, bf16[256,2048]{1,0:T(8,128)(2,1)}, u32[]{:S(2)}) copy-start(bf16[256,2048]{1,0:T(8,128)(2,1)} %param.23) | copy-start | bytes 3145732
  119.1 2.2 copy-start.2
  179.0 0.7 copy-start.5
  222.1 18.7 %copy-start.3 = (bf16[128,2048]{1,0:T(8,128)(2,1)}, bf16[128,2048]{1,0:T(8,128)(2,1)S(1)}, u32[]{:S(2)}) copy-start(bf16[128,2048]{1,0:T(8,128)(2,1)S(1)} %fusion.14) | copy-start | bytes 1572868
  247.6 0.9 copy-start.6
Sparse Core Ops, SparseCore 0:
  179.1 41.7 reduce-scatter.1

commit v3 on v2

--- a/solution.py
+++ b/solution.py
@@ -485,12 +485,10 @@
     gate_proj = jnp.dot(shard_part, gate_weight, preferred_element_type=jnp.float32)
     lifted = jnp.dot(shard_part, up_weight, preferred_element_type=jnp.float32)
     hidden_act = (jax.nn.silu(gate_proj) * lifted).astype(jnp.bfloat16)
-    summed = lax.psum_scatter(
-        jnp.dot(hidden_act, down_weight, preferred_element_type=jnp.float32).astype(jnp.bfloat16),
-        "req",
-        scatter_dimension=0,
-        tiled=True,
-    ).astype(jnp.float32)
+    shares = jnp.dot(hidden_act, down_weight, preferred_element_type=jnp.float32)
+    shares = shares.astype(jnp.bfloat16).reshape(owner_count, tok_rows, -1)
+    shares = exchange(shares, True, owners, 5, "mlp_exchange")
+    summed = jnp.sum(shares.astype(jnp.float32), axis=0)
     final_state = (middle.astype(jnp.float32) + summed).astype(jnp.bfloat16)
     local_index = jnp.arange(tok_rows) + tok_place * tok_rows
     picker = (local_index[None, :] == (end_rows - 1)[:, None]).astype(jnp.bfloat16)

time: 260 us -> 258 us (level); the launches traced: 255 us -> 257 us
  Pallas kernels: 138 us -> 187 us
  waiting for transfers between devices: 40.3 us -> 0.01 us
  between operations: 14.3 us -> 0.95 us
  other arithmetic: 16.9 us -> 22.7 us
    pallas_call x5 -> x6, Pallas kernels: 110 us -> 153 us  [remote_call(): pl.pallas_call(body, out_shape=outputs, in_specs=[pl.BlockSpec(memory_spa...]
    reduce_scatter x1 -> x0, waiting for transfers between devices: 40.3 us -> none  [shards(): lax.psum_scatter(jnp.dot(hidden_act, down_weight, preferred_element_type=...]
    pallas_call x1, Pallas kernels: 27.5 us -> 33.8 us  [attention(): pl.pallas_call(lambda *refs: attention_kernel(member_count, heads, piece,...]
  transfers between devices with their start and end apart: 5 -> 4, of which waited for: 1 -> 0; matrix products, arithmetic and copies ran while one was open for 8% -> 10% of each run, Pallas kernels for 24% -> 26%
where the time goes in v3:
time: 258 us; the launch traced here: 257 us
  Pallas kernels  187 us (72%)
  matrix products  38 us (15%)
  other arithmetic  22.7 us (9%)
  local copies, waits for them, and re-layouts  7.73 us (3%)
    pallas_call x6, Pallas kernels, remote_call(): pl.pallas_call(body, out_shape=outputs, in_specs=[pl.BlockSpec(memory_spa...  153 us
    pallas_call x1, Pallas kernels, attention(): pl.pallas_call(lambda *refs: attention_kernel(member_count, heads, piece,...  33.8 us
    dot_general x1, matrix products, shards(): jnp.dot(hidden_act, down_weight, preferred_element_type=jnp.float32)  10.6 us
    dot_general x1, matrix products, shards(): lax.dot_general(final_normed, head_weight, (((1,), (1,)), ((), ())), pref...  10.1 us
    dot_general x1, matrix products, shards(): jnp.dot(shard_part, gate_weight, preferred_element_type=jnp.float32)  6.49 us
  transfers between devices with their start and end apart: 4, of which 0 were waited for; matrix products, arithmetic and copies ran while one was open for 10% of the time, Pallas kernels for 26%

profile of v3, /device:TPU:9, one launch (start us, length us, event | category | flops | bytes accessed | tf_op | source)
XLA Modules:
  0.0 257.2 jit_solution(6221498871174519587)
XLA Ops:
  2.0 0.8 reduce-window.4
  3.5 1.2 fusion.7
  5.4 2.0 fusion.9.rows_ref
  7.4 33.1 %front_exchange.1 = (bf16[4,128,2048]{2,1,0:T(8,128)(2,1)}, bf16[8,128,128]{2,1,0:T(8,128)(2,1)}, bf16[4,8,128,128]{3,2,1,0:T(8,128)(2,1)}) custom-call(bf16[128,2048]{1,0:T(8,128)(2,1)} %fusion.9.rows_ref, bf16[8,128,128]{2,1,0:T(8,128)(2,1)} %bitcast.74), custom_call_target="tpu_custom_call" | custom-call | tf_op jit(solution)/shard_map/front_exchange/pallas_call | solution.py:240
  40.6 2.5 fusion.15
  43.3 1.0 fusion.23
  45.9 0.9 select_reduce_fusion.1
  46.8 1.0 multiply_sine_fusion.1
  47.7 1.2 broadcast_add_fusion
  49.8 0.8 copy.34
  51.9 1.2 maximum_dynamic-update-slice_fusion
  53.2 1.7 copy.37
  54.8 0.9 constant_dynamic-update-slice_fusion
  55.8 0.8 constant_dynamic-slice_fusion
  56.6 1.7 copy.33
  58.3 3.5 %fusion.refs_1_ = f32[512,512]{1,0:T(8,128)S(1)} fusion(bf16[512,2048]{1,0:T(8,128)(2,1)} %bitcast.67, bf16[2048,256]{1,0:T(8,128)(2,1)} %collective-permute-done, bf16[2048,256]{1,0:T(8,128)(2,1)} %param.21), kind=kOutput, calls=%fused_computation.5 | convolution fusion | flops 1077936128 | bytes 5242880 | tf_op jit(solution)/shard_map/dot_general | solution.py:453
  61.9 33.8 %attention.1 = bf16[512,512]{1,0:T(8,128)(2,1)S(1)} custom-call(s32[13]{0:T(128)S(1)} %pad_add_fusion.refs_0_, f32[512,512]{1,0:T(8,128)S(1)} %fusion.refs_1_, f32[32,512]{1,0:T(8,128)S(1)} %get-tuple-element.27.refs_2_, f32[32,512]{1,0:T(8,128)S(1)} %get-tuple-element.26.refs_3_, bf16[4,1024,128]{2,1,0:T(8,128)(2,1)S(1)} %bitcast.63, ...), custom_call_target="tpu_custom_call" | custom-call | flops 20000000000 | bytes 8000000 | tf_op jit(solution)/shard_map/attention/pallas_call | solution.py:168
  95.7 3.9 %convolution_convert_fusion.1 = bf16[512,2048]{1,0:T(8,128)(2,1)} fusion(bf16[512,512]{1,0:T(8,128)(2,1)S(1)} %attention.1, bf16[256,2048]{1,0:T(8,128)(2,1)} %collective-permute-done.3, bf16[256,2048]{1,0:T(8,128)(2,1)S(1)} %copy-done.10), kind=kOutput, calls=%fused_computation.3 | convolution fusion | flops 1078984704 | bytes 4718592 | tf_op jit(solution)/shard_map/dot_general | solution.py:473
  99.6 22.7 %out_exchange.1 = bf16[4,128,2048]{2,1,0:T(8,128)(2,1)} custom-call(bf16[4,128,2048]{2,1,0:T(8,128)(2,1)} %bitcast.68), custom_call_target="tpu_custom_call" | custom-call | tf_op jit(solution)/shard_map/out_exchange/pallas_call | solution.py:240
  122.3 2.1 convert_reduce_fusion.1
  124.7 1.0 fusion.13.source
  125.7 35.9 %mlp_gather.1 = bf16[4,128,2048]{2,1,0:T(8,128)(2,1)} custom-call(bf16[128,2048]{1,0:T(8,128)(2,1)} %fusion.13.source), custom_call_target="tpu_custom_call" | custom-call | tf_op jit(solution)/shard_map/mlp_gather/pallas_call | solution.py:240
  161.6 6.5 %fusion.48 = f32[512,1024]{1,0:T(8,128)} fusion(bf16[512,2048]{1,0:T(8,128)(2,1)} %bitcast.64, bf16[2048,1024]{1,0:T(8,128)(2,1)} %param.25), kind=kOutput, calls=%fused_computation.97 | convolution fusion | flops 2147483648 | bytes 8388608 | tf_op jit(solution)/shard_map/dot_general | solution.py:485
  168.1 10.6 %convolution_convert_fusion = bf16[512,2048]{1,0:T(8,128)(2,1)} fusion(bf16[1024,2048]{1,0:T(8,128)(2,1)} %param.27, f32[512,1024]{1,0:T(8,128)} %fusion.48, bf16[512,2048]{1,0:T(8,128)(2,1)} %bitcast.65, bf16[2048,1024]{1,0:T(8,128)(2,1)} %param.26), kind=kOutput, calls=%fused_computation.2 | convolution fusion | flops 4299161600 | bytes 14680064 | tf_op jit(solution)/shard_map/dot_general | solution.py:488
  178.8 48.9 %mlp_exchange.1 = bf16[4,128,2048]{2,1,0:T(8,128)(2,1)} custom-call(bf16[4,128,2048]{2,1,0:T(8,128)(2,1)} %bitcast.69), custom_call_target="tpu_custom_call" | custom-call | tf_op jit(solution)/shard_map/mlp_exchange/pallas_call | solution.py:240
  227.7 2.1 convert_reduce_fusion
  230.0 0.8 convolution_convert_fusion.2.source
  230.8 6.9 %last_exchange.1 = bf16[8,4,2048]{2,1,0:T(4,128)(2,1)} custom-call(bf16[4,2048]{1,0:T(4,128)(2,1)} %convolution_convert_fusion.2.source), custom_call_target="tpu_custom_call" | custom-call | tf_op jit(solution)/shard_map/last_exchange/pallas_call | solution.py:240
  237.8 1.0 convert_reduce_fusion.2
  239.4 10.1 %fusion.47 = (f32[4]{0:T(128)S(1)}, f32[4,4000]{1,0:T(4,128)S(1)}) fusion(bf16[4000,2048]{1,0:T(8,128)(2,1)} %param.29, f32[4,2048]{1,0:T(4,128)S(1)} %convert_reduce_fusion.2, f32[2048]{0:T(1024)S(1)} %convert_element_type.101, f32[4]{0:T(128)S(1)} %get-tuple-element.28), kind=kOutput, calls=%fused_computation.96 | convolution fusion | flops 65576572 | bytes 16488992 | tf_op jit(solution)/shard_map/dot_general | solution.py:503
  250.4 5.1 %tail_exchange.1 = f32[8,8,128]{2,1,0:T(8,128)} custom-call(f32[8,128]{1,0:T(8,128)} %select_maximum_fusion.source), custom_call_target="tpu_custom_call" | custom-call | tf_op jit(solution)/shard_map/tail_exchange/pallas_call | solution.py:240
  255.5 0.9 fusion.46
  (56 shorter events, 9.6 us)
Async XLA Ops:
  0.6 40.0 %copy-start = (bf16[4,2048,128]{2,1,0:T(8,128)(2,1)S(1)}, bf16[4,2048,128]{2,1,0:T(8,128)(2,1)}, u32[]{:S(2)}) copy-start(bf16[4,2048,128]{2,1,0:T(8,128)(2,1)} %param.22) | copy-start | bytes 6291460
  0.6 57.7 %collective-permute-start = (bf16[2048,256]{1,0:T(8,128)(2,1)}, bf16[2048,256]{1,0:T(8,128)(2,1)}, u32[]{:S(2)}, u32[]{:S(2)}) collective-permute-start(bf16[2048,256]{1,0:T(8,128)(2,1)} %param.21), channel_id=1, source_target_pairs={{1,0},{0,1},{3,2},{2,3},{5,4},{4,5},{7,6},{6,7},{9,8},{8,9},{11,10... | collective-permute-start | bytes 3145736 | tf_op jit(solution)/shard_map/ppermute | solution.py:408
  1.4 94.3 %collective-permute-start.3 = (bf16[256,2048]{1,0:T(8,128)(2,1)}, bf16[256,2048]{1,0:T(8,128)(2,1)}, u32[]{:S(2)}, u32[]{:S(2)}) collective-permute-start(bf16[256,2048]{1,0:T(8,128)(2,1)} %param.23), channel_id=1, source_target_pairs={{1,0},{0,1},{3,2},{2,3},{5,4},{4,5},{7,6},{6,7},{9,8},{8,9},{11,10... | collective-permute-start | bytes 3145736 | tf_op jit(solution)/shard_map/ppermute | solution.py:408
  40.6 4.4 %copy-start.1 = (bf16[4,8,128,128]{3,2,1,0:T(8,128)(2,1)S(1)}, bf16[4,8,128,128]{3,2,1,0:T(8,128)(2,1)}, u32[]{:S(2)}) copy-start(bf16[4,8,128,128]{3,2,1,0:T(8,128)(2,1)} %get-tuple-element.8) | copy-start | bytes 3145732
  40.6 10.7 %copy-start.5 = (bf16[2048]{0:T(1024)(128)(2,1)S(1)}, bf16[2048]{0:T(1024)(128)(2,1)}, u32[]{:S(2)}) copy-start(bf16[2048]{0:T(1024)(128)(2,1)} %param.24) | copy-start | bytes 12292
  40.6 11.3 %copy-start.6 = (bf16[2048]{0:T(1024)(128)(2,1)S(1)}, bf16[2048]{0:T(1024)(128)(2,1)}, u32[]{:S(2)}) copy-start(bf16[2048]{0:T(1024)(128)(2,1)} %param.28) | copy-start | bytes 12292
  44.9 8.3 %collective-permute-start.2 = (bf16[512,128]{0,1:T(8,128)(2,1)}, bf16[512,128]{0,1:T(8,128)(2,1)}, u32[]{:S(2)}, u32[]{:S(2)}) collective-permute-start(bf16[512,128]{0,1:T(8,128)(2,1)} %pad_maximum_fusion), channel_id=1, source_target_pairs={{1,0},{0,1},{3,2},{2,3},{5,4},{4,5},{7,6},{6,7},{9,8},{8,9},{11,10... | collective-permute-start | bytes 393224 | tf_op jit(solution)/shard_map/ppermute | solution.py:408
  45.0 16.9 %collective-permute-start.1 = (bf16[4,1024,128]{2,1,0:T(8,128)(2,1)S(1)}, bf16[4,1024,128]{2,1,0:T(8,128)(2,1)}, u32[]{:S(2)}, u32[]{:S(2)}) collective-permute-start(bf16[4,1024,128]{2,1,0:T(8,128)(2,1)S(1)} %bitcast.62), channel_id=1, source_target_pairs={{1,0},{0,1},{3,2},{2,3},{5,4},{4,5},{7,6},{6,7},{9,8},{8,9},{11,10... | collective-permute-start | bytes 3145736 | tf_op jit(solution)/shard_map/ppermute | solution.py:408
  61.9 33.9 %copy-start.10 = (bf16[256,2048]{1,0:T(8,128)(2,1)S(1)}, bf16[256,2048]{1,0:T(8,128)(2,1)}, u32[]{:S(2)}) copy-start(bf16[256,2048]{1,0:T(8,128)(2,1)} %param.23) | copy-start | bytes 3145732
  122.3 2.2 copy-start.2
  122.3 2.4 copy-start.4
  227.7 2.3 copy-start.8
  227.7 2.3 copy-start.9
  230.0 19.6 %copy-start.3 = (bf16[128,2048]{1,0:T(8,128)(2,1)}, bf16[128,2048]{1,0:T(8,128)(2,1)S(1)}, u32[]{:S(2)}) copy-start(bf16[128,2048]{1,0:T(8,128)(2,1)S(1)} %fusion.14) | copy-start | bytes 1572868
  256.4 0.9 copy-start.7
